TPU v7x, 128 devices: a whole 4x4x4 slice. The times are simulated.
128 devices in a mesh: mem: 4 (over y), col: 32 (over z, x, core).
Axes of the slice: x: 4, y: 4, z: 4, core: 2. Of those that a mesh axis runs over, the one named last changes fastest.
Arguments:
- ensemble: bfloat16 [256, 3, 128, 4096], P('mem', None, None, 'col'), may hold values from -6 to 6
- increment: bfloat16 [3, 128, 4096], P(None, 'mem', 'col'), may hold values from -6 to 6
- vert_root: bfloat16 [3, 128, 128], replicated, may hold values from -1 to 2, as said below
- tiles: bfloat16 [32, 8, 128, 128], replicated, may hold values from -2 to 3, as said below
- tile_col: int32 [32, 8], replicated, may hold values from 0 to 31
- level_reach: int32 [128], replicated, may hold values from 2 to 8, as said below
Outputs:
- covaried: bfloat16 [3, 128, 4096], P(None, 'mem', 'col')
Inputs may be any that keep to these rules, and one draw needn't show every extreme that they name: `vert_root`: each variable's matrix is the identity plus bounded noise. `tiles`: slot 0 of block row r is the identity plus bounded noise; the other slots are bounded noise. `level_reach`: level 0 uses 2 slots and the top level uses all 8; the count mostly rises with the level.
All inputs are finite; a program needn't handle non-finite values.
Results may differ from a plain program's by a relative error of at most 0.012.
Values may be sent and summed in bfloat16 or wider, within the bound.
No kernel may reach another device: no remote copies, remote signals or barrier semaphores. Data moves between devices by JAX's collectives and lax.ppermute only.
A program may use at most 128 MiB of HBM per device.

v0:
```python
import jax
import jax.numpy as jnp
from jax import lax
from jax.sharding import PartitionSpec as P


def on_device(ensemble, increment, vert_root, tiles, tile_col, level_reach):
    columns_axis = lax.axis_size("col")
    members_all = ensemble.shape[0] * lax.axis_size("mem")
    levels = vert_root.shape[1]
    local_levels = levels // columns_axis
    n_blocks = tiles.shape[0]
    width = tiles.shape[2]
    col_index = lax.axis_index("col")
    whole_incr = lax.all_gather(increment, "mem", axis=1, tiled=True)
    weighted_increment = (
        ensemble.astype(jnp.float32) * whole_incr.astype(jnp.float32)[None]
    ).astype(jnp.bfloat16)
    position = jnp.arange(levels, dtype=jnp.int32)
    within = jnp.arange(local_levels, dtype=jnp.int32)
    mine = col_index * local_levels + within
    sorted_vertical_factor = jnp.take(vert_root, position, axis=2)
    lifted_increment = jnp.einsum(
        "vkq,mvkc->mvqc",
        sorted_vertical_factor,
        weighted_increment,
        preferred_element_type=jnp.float32,
    ).astype(jnp.bfloat16)
    reach_mine = jnp.take(level_reach, mine)
    gathered = lax.all_to_all(lifted_increment, "col", split_axis=2, concat_axis=3, tiled=True)
    items = gathered.shape[0]
    row_count = items * gathered.shape[1]
    planes = gathered.reshape(row_count, local_levels, n_blocks, width)

    def level_step(level, result):
        plane = lax.dynamic_index_in_dim(planes, level, 1, keepdims=False)

        def slot_step(slot, acc):
            sources = lax.dynamic_index_in_dim(tile_col, slot, 1, keepdims=False)
            picked = jnp.take(plane, sources, axis=1)
            blocks = lax.dynamic_index_in_dim(tiles, slot, 1, keepdims=False)
            return acc + jnp.einsum(
                "rbi,bij->rbj", picked, blocks, preferred_element_type=jnp.float32
            )

        summed = lax.fori_loop(
            0, reach_mine[level], slot_step, jnp.zeros((row_count, n_blocks, width), jnp.float32)
        )
        return lax.dynamic_update_index_in_dim(result, summed.astype(jnp.bfloat16), level, 1)

    spread_increment = lax.fori_loop(
        0,
        local_levels,
        level_step,
        jnp.zeros((row_count, local_levels, n_blocks, width), jnp.bfloat16),
    )
    spread_increment = spread_increment.reshape(gathered.shape)
    returned_increment = lax.all_to_all(
        spread_increment, "col", split_axis=3, concat_axis=2, tiled=True
    )
    lowered_increment = jnp.einsum(
        "vlq,mvqc->mvlc",
        sorted_vertical_factor,
        returned_increment,
        preferred_element_type=jnp.float32,
    )
    partial_sum = jnp.sum(ensemble.astype(jnp.float32) * lowered_increment, axis=0)
    summed_all = lax.psum(partial_sum.astype(jnp.bfloat16), "mem").astype(jnp.float32)
    group_levels = levels // lax.axis_size("mem")
    share = lax.dynamic_slice_in_dim(
        summed_all, lax.axis_index("mem") * group_levels, group_levels, 1
    )
    return (share / (members_all - 1)).astype(jnp.bfloat16)


def solution(mesh):
    placed = (P("mem", None, None, "col"), P(None, "mem", "col"), P(), P(), P(), P())
    return jax.shard_map(
        on_device, mesh=mesh, in_specs=placed, out_specs=P(None, "mem", "col"), check_vma=False
    )
```

profile of v0, /device:TPU:0, one launch (start us, length us, event | category | flops | bytes accessed | tf_op | source)
XLA Modules:
  0.0 595.2 jit_solution(10978426257841573920)
XLA Ops:
  6.6 8.7 %copy.68 = bf16[64,3,128,128]{2,3,0,1:T(8,128)(2,1)} copy(bf16[64,3,128,128]{3,2,1,0:T(8,128)(2,1)} %param.10) | data formatting | bytes 12582912 | tf_op args[0]
  16.5 12.6 %all_gather.3 = bf16[3,128,128]{2,1,0:T(8,128)(2,1)S(1)} all-gather(bf16[3,32,128]{2,1,0:T(8,128)(2,1)S(1)} %copy-done.5), channel_id=1, replica_groups=mesh['mem'=4,'col'=32] {'mem'}, dimensions={1}, use_global_device_ids=true | all-gather | bytes 122880 | tf_op jit(solution)/shard_map/all_gather | solution.py:15
  29.2 7.3 %convert_bitcast_fusion.1 = bf16[64,3,128,128]{2,3,0,1:T(8,128)(2,1)} fusion(bf16[3,128,128,1]{2,1,3,0:T(8,128)(2,1)S(1)} %copy.84, bf16[64,3,128,128]{2,3,0,1:T(8,128)(2,1)} %copy.68, f32[3,128,128]{1,2,0:T(8,128)S(1)} %copy.69), kind=kOutput, calls=%fused_computation.26 | convolution fusion | flops 817889280 | bytes 12877824 | tf_op jit(solution)/shard_map/vkq,mvkc->mvqc/dot_general | solution.py:23
  36.5 9.0 %copy.72 = bf16[64,3,128,128]{3,0,1,2:T(8,128)(2,1)} copy(bf16[64,3,128,128]{2,3,0,1:T(8,128)(2,1)} %convert_bitcast_fusion.1) | data formatting | bytes 12582912 | tf_op jit(solution)/shard_map/convert_element_type | solution.py:28
  45.5 8.2 %all-to-all-start = ((bf16[64,3,128,128]{3,0,1,2:T(8,128)(2,1)}), bf16[64,3,128,128]{3,0,1,2:T(8,128)(2,1)}, u32[]{:S(2)}, u32[]{:S(2)}) async-start(bf16[64,3,128,128]{3,0,1,2:T(8,128)(2,1)} %copy.72), calls=%async_computation | async-start | bytes 12582912 | tf_op jit(solution)/shard_map/all_to_all | solution.py:30
  54.0 10.3 %copy.76 = bf16[32,8,128,128]{3,2,0,1:T(8,128)(2,1)} copy(bf16[32,8,128,128]{3,2,1,0:T(8,128)(2,1)} %param.13) | data formatting | bytes 16777216 | tf_op jit(solution)/shard_map/while | solution.py:51
  65.0 66.7 %all-to-all-done = bf16[64,3,128,128]{3,0,1,2:T(8,128)(2,1)} async-done(((bf16[64,3,128,128]{3,0,1,2:T(8,128)(2,1)}), bf16[64,3,128,128]{3,0,1,2:T(8,128)(2,1)}, u32[]{:S(2)}, u32[]{:S(2)}) %all-to-all-start) | async-done | bytes 6291488 | tf_op jit(solution)/shard_map/all_to_all | solution.py:30
  131.7 9.5 %copy.74 = bf16[64,3,4,32,128]{4,3,2,1,0:T(8,128)(2,1)} copy(bf16[64,3,4,32,128]{4,0,1,2,3:T(8,128)(2,1)} %bitcast.14) | data formatting | bytes 12582912 | tf_op jit(solution)/shard_map/all_to_all | solution.py:30
  141.1 94.5 %while.36 = (s32[]{:T(128)}, bf16[192,4,32,128]{3,2,1,0:T(8,128)(2,1)}, s32[4]{0:T(128)S(1)}, bf16[192,4,32,128]{3,2,1,0:T(8,128)(2,1)}, bf16[32,8,128,128]{3,2,...) while((s32[]{:T(128)}, ...), condition=%wide.region_3.4_spmd, body=%wide.region_0.3_spmd.sunk | while | flops 203687104 | bytes 29365664 | solution.py:51
  146.2 14.2 %while.37 = (s32[]{:T(128)}, f32[192,32,128]{2,0,1:T(8,128)}, s32[]{:T(128)}, bf16[32,8,128,128]{3,2,0,1:T(8,128)(2,1)}, s32[32,8]{0,1:T(8,128)}, /*index=5*/bf1...) while((s32[]{:T(128)}, f32[192,32,128]{2,0,1:T(8,128)}, s32[]{:T(128)}, ...), condition=%wide.region_2.2_spmd, body=%wide.region_1.1_spmd.sunk | while | flops 202900672 | bytes 12063431 | solution.py:46
  169.8 14.2 %while.37 = (s32[]{:T(128)}, f32[192,32,128]{2,0,1:T(8,128)}, s32[]{:T(128)}, bf16[32,8,128,128]{3,2,0,1:T(8,128)(2,1)}, s32[32,8]{0,1:T(8,128)}, /*index=5*/bf1...) while((s32[]{:T(128)}, f32[192,32,128]{2,0,1:T(8,128)}, s32[]{:T(128)}, ...), condition=%wide.region_2.2_spmd, body=%wide.region_1.1_spmd.sunk | while | flops 202900672 | bytes 12063431 | solution.py:46
  171.9 4.7 bitcast_add_fusion.2
  193.4 14.2 %while.37 = (s32[]{:T(128)}, f32[192,32,128]{2,0,1:T(8,128)}, s32[]{:T(128)}, bf16[32,8,128,128]{3,2,0,1:T(8,128)(2,1)}, s32[32,8]{0,1:T(8,128)}, /*index=5*/bf1...) while((s32[]{:T(128)}, f32[192,32,128]{2,0,1:T(8,128)}, s32[]{:T(128)}, ...), condition=%wide.region_2.2_spmd, body=%wide.region_1.1_spmd.sunk | while | flops 202900672 | bytes 12063431 | solution.py:46
  195.6 4.7 bitcast_add_fusion.2
  217.0 14.2 %while.37 = (s32[]{:T(128)}, f32[192,32,128]{2,0,1:T(8,128)}, s32[]{:T(128)}, bf16[32,8,128,128]{3,2,0,1:T(8,128)(2,1)}, s32[32,8]{0,1:T(8,128)}, /*index=5*/bf1...) while((s32[]{:T(128)}, f32[192,32,128]{2,0,1:T(8,128)}, s32[]{:T(128)}, ...), condition=%wide.region_2.2_spmd, body=%wide.region_1.1_spmd.sunk | while | flops 202900672 | bytes 12063431 | solution.py:46
  219.2 4.7 bitcast_add_fusion.2
  235.6 9.7 %reshape.38 = bf16[64,3,4,4096]{3,2,1,0:T(4,128)(2,1)} reshape(bf16[192,4,32,128]{3,2,1,0:T(8,128)(2,1)} %get-tuple-element.147) | data formatting | bytes 12582912 | tf_op jit(solution)/shard_map/reshape | solution.py:57
  245.3 20.2 %copy.78 = bf16[64,3,4,4096]{0,2,1,3:T(4,128)(2,1)} copy(bf16[64,3,4,4096]{3,2,1,0:T(4,128)(2,1)} %reshape.38) | data formatting | bytes 12582912 | tf_op jit(solution)/shard_map/reshape | solution.py:57
  265.5 24.2 %reshape.65 = bf16[32,2,49152]{2,1,0:T(2,128)(2,1)} reshape(bf16[4096,3,4,64]{3,2,1,0:T(4,128)(2,1)} %bitcast.60) | data formatting | bytes 12582912
  289.7 205.0 %all_to_all.33 = bf16[32,2,49152]{2,1,0:T(2,128)(2,1)} all-to-all(bf16[32,2,49152]{2,1,0:T(2,128)(2,1)} %reshape.65), channel_id=1, replica_groups=mesh['mem'=4,'col'=32] {'col'}, dimensions={0} | all-to-all | bytes 12582912 | tf_op jit(solution)/shard_map/all_to_all | solution.py:58
  494.7 23.5 %reshape.66 = bf16[4096,3,4,64]{3,2,1,0:T(4,128)(2,1)} reshape(bf16[32,2,49152]{2,1,0:T(2,128)(2,1)} %all_to_all.33) | data formatting | bytes 12582912
  518.2 17.9 %copy.90 = bf16[64,3,4,32,128]{4,0,2,3,1:T(8,128)(2,1)} copy(bf16[64,3,4,32,128]{0,2,1,4,3:T(4,128)(2,1)} %bitcast.61) | data formatting | bytes 12582912 | tf_op jit(solution)/shard_map/all_to_all | solution.py:58
  536.1 10.8 %fusion.9 = bf16[3,128,128]{1,2,0:T(8,128)(2,1)S(1)} fusion(bf16[64,3,128,128]{2,3,0,1:T(8,128)(2,1)} %copy.68, bf16[3,128,128,1]{2,1,3,0:T(8,128)(2,1)S(1)} %copy-done.3, bf16[64,3,128,128]{3,0,2,1:T(8,128)(2,1)} %bitcast.63), kind=kOutput, calls=%fused_computation.22 | convolution fusion | flops 814694400 | bytes 12779520 | tf_op jit(solution)/shard_map/vlq,mvqc->mvlc/dot_general | solution.py:61
  547.7 39.3 %all-reduce.2.cloned.1.call-done = bf16[3,128,128]{2,1,0:T(8,128)(2,1)} async-done(((bf16[3,128,128]{2,1,0:T(8,128)(2,1)}), bf16[3,128,128]{2,1,0:T(8,128)(2,1)}) %all-reduce.2.cloned.1.call-update) | async-done | bytes 98320 | tf_op jit(solution)/shard_map/psum | solution.py:68
  (82 shorter events, 77.7 us)
Async XLA Ops:
  6.5 57.8 %copy-start = (s32[128]{0:T(128)S(1)}, s32[128]{0:T(128)}, u32[]{:S(2)}) copy-start(s32[128]{0:T(128)} %param.15) | copy-start | bytes 1540
  6.5 8.7 %copy-start.4 = (bf16[3,128,128]{2,1,0:T(8,128)(2,1)S(1)}, bf16[3,128,128]{2,1,0:T(8,128)(2,1)}, u32[]{:S(2)}) copy-start(bf16[3,128,128]{2,1,0:T(8,128)(2,1)} %param.12) | copy-start | bytes 294916
  6.5 9.9 %copy-start.5 = (bf16[3,32,128]{2,1,0:T(8,128)(2,1)S(1)}, bf16[3,32,128]{2,1,0:T(8,128)(2,1)}, u32[]{:S(2)}) copy-start(bf16[3,32,128]{2,1,0:T(8,128)(2,1)} %param.11) | copy-start | bytes 73732
  16.5 20.0 %copy-start.2 = (bf16[3,128,128,1]{2,1,3,0:T(8,128)(2,1)}, bf16[3,128,128,1]{2,1,3,0:T(8,128)(2,1)S(1)}, u32[]{:S(2)}) copy-start(bf16[3,128,128,1]{2,1,3,0:T(8,128)(2,1)S(1)} %copy.84) | copy-start | bytes 294916
  45.5 86.1 %all-to-all-start = ((bf16[64,3,128,128]{3,0,1,2:T(8,128)(2,1)}), bf16[64,3,128,128]{3,0,1,2:T(8,128)(2,1)}, u32[]{:S(2)}, u32[]{:S(2)}) async-start(bf16[64,3,128,128]{3,0,1,2:T(8,128)(2,1)} %copy.72), calls=%async_computation | async-start | bytes 12582912 | tf_op jit(solution)/shard_map/all_to_all | solution.py:30
  53.8 533.3 %all-reduce.2.cloned.1.call-start = ((), (), s32[]{:S(2)}) async-start(), calls=%async_computation.2 | async-start | bytes 196608 | tf_op jit(solution)/shard_map/psum | solution.py:68
  518.2 17.9 %copy-start.3 = (bf16[3,128,128,1]{2,1,3,0:T(8,128)(2,1)S(1)}, bf16[3,128,128,1]{2,1,3,0:T(8,128)(2,1)}, u32[]{:S(2)}) copy-start(bf16[3,128,128,1]{2,1,3,0:T(8,128)(2,1)} %copy-done.2) | copy-start | bytes 294916
  536.1 52.3 %copy-start.1 = (s32[128]{0:T(128)S(1)}, s32[128]{0:T(128)}, u32[]{:S(2)}) copy-start(s32[128]{0:T(128)} %param.15) | copy-start | bytes 1540
Sparse Core Ops, SparseCore 0:
  547.8 39.1 all-reduce.1
where the time goes:
time: 600 us; the launch traced here: 595 us
  blocking collectives  218 us (36%)
  local copies, waits for them, and re-layouts  171 us (28%)
  waiting for transfers between devices  106 us (18%)
  matrix products  55.6 us (9%)
  other arithmetic  15.8 us (3%)
  between operations  13.5 us (2%)
  starting transfers between devices  8.47 us (1%)
  loops' own time  6.95 us (1%)
    all_to_all x1, blocking collectives, on_device(): lax.all_to_all(spread_increment, 'col', split_axis=3, concat_axis=2, tile...  205 us
    all_to_all x1, waiting for transfers between devices, on_device(): lax.all_to_all(lifted_increment, 'col', split_axis=2, concat_axis=3, tile...  66.7 us
    unnamed x16, local copies, waits for them, and re-layouts  56.5 us
    psum x1, waiting for transfers between devices, on_device(): lax.psum(partial_sum.astype(jnp.bfloat16), 'mem').astype(jnp.float32)  39.3 us
    dot_general x8, matrix products, slot_step(): jnp.einsum('rbi,bij->rbj', picked, blocks, preferred_element_type=jnp.flo...  37.5 us
    reshape x2, local copies, waits for them, and re-layouts, on_device(): spread_increment = spread_increment.reshape(gathered.shape)  29.9 us
    all_to_all x1, local copies, waits for them, and re-layouts, on_device(): lax.all_to_all(spread_increment, 'col', split_axis=3, concat_axis=2, tile...  17.9 us
    all_gather x1, blocking collectives, on_device(): whole_incr = lax.all_gather(increment, 'mem', axis=1, tiled=True)  12.6 us
  transfers between devices with their start and end apart: 2, of which 2 were waited for; matrix products, arithmetic and copies ran while one was open for 2% of the time, Pallas kernels for 0%

commit v1 on v0

v1 whole, which is shorter than its diff:
```python
import functools

import jax
import jax.numpy as jnp
from jax import lax
from jax.experimental import pallas as pl
from jax.experimental.pallas import tpu as pltpu
from jax.sharding import PartitionSpec as P

BF = jnp.bfloat16
F32 = jnp.float32
CORES = 2


def member_kernel(
    where_ref, cols_ref, ens_ref, mine_ref, other_ref, vt_ref, vn_ref, mask_ref, tiles_ref,
    near_ref, far_ref, tile_buf, lifted, sems, *, var, slot_of_var,
):
    members = ens_ref.shape[1]
    n_blocks = ens_ref.shape[0]
    levels = ens_ref.shape[3]
    width = ens_ref.shape[4]
    y_n, z_n, x_n = mine_ref.shape[0], mine_ref.shape[1], mine_ref.shape[2]
    part_l = mine_ref.shape[4]
    slots = cols_ref.shape[1]
    pairs = slots // 2
    my_y, my_z, my_x, my_c = where_ref[0], where_ref[1], where_ref[2], where_ref[3]
    n_copies = sems.shape[0]
    per_copy = n_blocks // n_copies

    def tile_copy(piece):
        span = pl.ds(piece * per_copy, per_copy)
        return pltpu.make_async_copy(tiles_ref.at[span], tile_buf.at[span], sems.at[piece])

    for piece in range(n_copies):
        tile_copy(piece).start()

    def seat_of(step):
        off_z, off_x = step // x_n, step % x_n
        z = lax.rem(my_z + off_z, z_n)
        x = lax.rem(my_x + off_x, x_n)
        return off_z, off_x, (z * x_n + x) * CORES

    def lift_block(source_ref, block, in_z, in_x):
        halves = []
        for m in range(members):
            bands = []
            for quarter in range(y_n):
                off_y = lax.rem(my_y - quarter + y_n, y_n)
                incr = source_ref[off_y, in_z, in_x, var].astype(F32)
                rows = ens_ref[block, m, slot_of_var, quarter * part_l:(quarter + 1) * part_l, :]
                bands.append((rows.astype(F32) * incr).astype(BF))
            halves.append(jnp.concatenate(bands, axis=0))
        weighted = jnp.concatenate(halves, axis=1)
        lift = jnp.dot(vt_ref[var], weighted, preferred_element_type=F32).astype(BF)
        for m in range(members):
            lifted[block, m * levels:(m + 1) * levels, :] = lift[:, m * width:(m + 1) * width]

    def lift_step(step, carry):
        off_z, off_x, base = seat_of(step)
        in_z = lax.rem(z_n - off_z, z_n)
        in_x = lax.rem(x_n - off_x, x_n)
        lift_block(mine_ref, base + my_c, in_z, in_x)
        lift_block(other_ref, base + 1 - my_c, in_z, in_x)
        return carry

    lax.fori_loop(0, n_blocks // CORES, lift_step, 0)
    for piece in range(n_copies):
        tile_copy(piece).wait()

    def spread_block(target_ref, block, off_z, off_x):
        acc = None
        for pair in range(pairs):
            first = lifted[cols_ref[block, 2 * pair]]
            second = lifted[cols_ref[block, 2 * pair + 1]]
            both = jnp.concatenate([first, second], axis=1)
            if pair > 0:
                both = both * mask_ref[pair - 1]
            term = jnp.dot(
                both, tile_buf[block, 2 * pair * width:2 * (pair + 1) * width, :],
                preferred_element_type=F32,
            )
            acc = term if acc is None else acc + term
        spread = acc.astype(BF)
        beside = jnp.concatenate(
            [spread[m * levels:(m + 1) * levels, :] for m in range(members)], axis=1
        )
        lowered = jnp.dot(vn_ref[var], beside, preferred_element_type=F32)
        total = None
        for m in range(members):
            term = ens_ref[block, m, slot_of_var].astype(F32) * lowered[:, m * width:(m + 1) * width]
            total = term if total is None else total + term
        total = total.astype(BF)
        for quarter in range(y_n):
            off_y = lax.rem(quarter - my_y + y_n, y_n)
            target_ref[off_y, off_z, off_x] = total[quarter * part_l:(quarter + 1) * part_l, :]

    def spread_step(step, carry):
        off_z, off_x, base = seat_of(step)
        spread_block(near_ref, base + my_c, off_z, off_x)
        spread_block(far_ref, base + 1 - my_c, off_z, off_x)
        return carry

    lax.fori_loop(0, n_blocks // CORES, spread_step, 0)


def on_device(
    ensemble, increment, vert_root, tiles, tile_col, level_reach, *, y_n, z_n, x_n
):
    columns = lax.axis_size("col")
    members_all = ensemble.shape[0] * lax.axis_size("mem")
    members = ensemble.shape[0] // columns
    n_var, levels, width = ensemble.shape[1:]
    part_l = increment.shape[1]
    slots = tiles.shape[1]
    col = lax.axis_index("col")
    my_y = lax.axis_index("mem")
    my_z, my_x, my_c = col // (x_n * CORES), (col // CORES) % x_n, col % CORES
    where = jnp.stack([my_y, my_z, my_x, my_c]).astype(jnp.int32)

    def seat(z, x, c):
        return ((z % z_n) * x_n + x % x_n) * CORES + c

    seats = [(z, x, c) for z in range(z_n) for x in range(x_n) for c in range(CORES)]

    def shift_y(a, s):
        return lax.ppermute(a, "mem", [(i, (i + s) % y_n) for i in range(y_n)])

    def shift_z(a, s):
        return lax.ppermute(a, "col", [(seat(*p), seat(p[0] + s, p[1], p[2])) for p in seats])

    def shift_x(a, s):
        return lax.ppermute(a, "col", [(seat(*p), seat(p[0], p[1] + s, p[2])) for p in seats])

    def swap(a):
        return lax.ppermute(a, "col", [(seat(*p), seat(p[0], p[1], 1 - p[2])) for p in seats])

    def collect(a, shift, n):
        return jnp.stack([a] + [shift(a, s) for s in range(1, n)])

    by_member = ensemble.reshape(columns, members, n_var, levels, width)
    groups = ((0, 1), (2,))
    arrived, where_var = [], {}
    for index, group in enumerate(groups):
        piece = by_member[:, :, group[0]:group[-1] + 1]
        if arrived:
            piece, arrived[-1] = lax.optimization_barrier((piece, arrived[-1]))
        arrived.append(lax.all_to_all(piece, "col", 0, 0))
        for place, var in enumerate(group):
            where_var[var] = (index, place)

    mine = collect(increment, shift_x, x_n)
    mine = collect(mine, shift_z, z_n)
    mine = collect(mine, shift_y, y_n)
    other = swap(mine)

    vert_t = jnp.swapaxes(vert_root, 1, 2)
    active = (
        jnp.arange(2, slots, dtype=jnp.int32)[:, None] < level_reach[None, :]
    ).astype(BF).reshape(slots // 2 - 1, 2, levels)
    active = jnp.swapaxes(active, 1, 2)
    mask = jnp.broadcast_to(
        active[:, None, :, :, None], (slots // 2 - 1, members, levels, 2, width)
    ).reshape(slots // 2 - 1, members * levels, 2 * width)
    flat_tiles = tiles.reshape(columns, slots * width, width)

    vmem = pl.BlockSpec(memory_space=pltpu.VMEM)
    smem = pl.BlockSpec(memory_space=pltpu.SMEM)
    out = jax.ShapeDtypeStruct((y_n, z_n, x_n, part_l, width), BF)

    def add(parts):
        total = parts[0].astype(F32)
        for p in parts[1:]:
            total = total + p.astype(F32)
        return total

    held = []
    for var in range(n_var):
        index, place = where_var[var]
        near, far = pl.pallas_call(
            functools.partial(member_kernel, var=var, slot_of_var=place),
            out_shape=(out, out),
            in_specs=[smem, smem, vmem, vmem, vmem, vmem, vmem, vmem,
                      pl.BlockSpec(memory_space=pl.ANY)],
            out_specs=(vmem, vmem),
            scratch_shapes=[
                pltpu.VMEM(flat_tiles.shape, BF),
                pltpu.VMEM((columns, members * levels, width), BF),
                pltpu.SemaphoreType.DMA((4,)),
            ],
            compiler_params=pltpu.CompilerParams(vmem_limit_bytes=40 << 20),
            name=f"members_{var}",
        )(where, tile_col, arrived[index], mine, other, vert_t, vert_root, mask, flat_tiles)
        chip = add([near, swap(far)]).astype(BF)
        held.append(add([chip[0]] + [shift_y(chip[s], s) for s in range(1, y_n)]).astype(BF))
    held = jnp.stack(held, axis=2)
    held = add([held[0]] + [shift_z(held[s], s) for s in range(1, z_n)]).astype(BF)
    held = add([held[0]] + [shift_x(held[s], s) for s in range(1, x_n)])
    return (held / (members_all - 1)).astype(BF)


def solution(mesh):
    y_n = mesh.shape["mem"]
    side = int(round((mesh.shape["col"] // CORES) ** 0.5))
    placed = (P("mem", None, None, "col"), P(None, "mem", "col"), P(), P(), P(), P())
    return jax.shard_map(
        functools.partial(on_device, y_n=y_n, z_n=side, x_n=side),
        mesh=mesh, in_specs=placed, out_specs=P(None, "mem", "col"), check_vma=False,
    )
```

time: 600 us -> 213 us (0.35)
  blocking collectives: 218 us -> 0 us
  local copies, waits for them, and re-layouts: 171 us -> 18 us
  matrix products: 55.6 us -> 0 us
  Pallas kernels: 0 us -> 52.5 us
  starting transfers between devices: 8.47 us -> 47.7 us
  waiting for transfers between devices: 106 us -> 89.6 us
  between operations: 13.5 us -> 0.31 us
  other arithmetic: 15.8 us -> 4 us
  loops' own time: 6.95 us -> 0 us
    all_to_all x1 -> x0, blocking collectives: 205 us -> none  [on_device(): lax.all_to_all(spread_increment, 'col', split_axis=3, concat_axis=2, tile...]
    ppermute x0 -> x28, waiting for transfers between devices: none -> 89.6 us  [the longest x6 52.1 us: shift_x(): lax.ppermute(a, 'col', [(seat(*p), seat(p[0], p[1] + s, p[2])) for p in s...]
    all_to_all x1 -> x2, waiting for transfers between devices: 66.7 us -> 0.01 us  [on_device(): arrived.append(lax.all_to_all(piece, 'col', 0, 0))]
    dot_general x10 -> x0, matrix products: 55.6 us -> none  [the longest x8 37.5 us: slot_step(): jnp.einsum('rbi,bij->rbj', picked, blocks, preferred_element_type=jnp.flo...]
    pallas_call x0 -> x3, Pallas kernels: none -> 52.5 us  [on_device(): pl.pallas_call(functools.partial(member_kernel, var=var, slot_of_var=plac...]
    unnamed x16 -> x28, local copies, waits for them, and re-layouts: 56.5 us -> 6.72 us
    psum x1 -> x0, waiting for transfers between devices: 39.3 us -> none  [on_device(): lax.psum(partial_sum.astype(jnp.bfloat16), 'mem').astype(jnp.float32)]
    ppermute x0 -> x28, starting transfers between devices: none -> 34.2 us  [the longest x12 15.5 us: shift_y(): return lax.ppermute(a, 'mem', [(i, (i + s) % y_n) for i in range(y_n)])]
  transfers between devices with their start and end apart: 2 -> 30, of which waited for: 2 -> 17; matrix products, arithmetic and copies ran while one was open for 2% -> 5% of each run, Pallas kernels for 0% -> 25%
where the time goes in v1:
time: 213 us; the launch traced here: 212 us
  waiting for transfers between devices  89.6 us (42%)
  Pallas kernels  52.5 us (25%)
  starting transfers between devices  47.7 us (22%)
  local copies, waits for them, and re-layouts  18 us (8%)
  other arithmetic  4 us (2%)
    pallas_call x3, Pallas kernels, on_device(): pl.pallas_call(functools.partial(member_kernel, var=var, slot_of_var=plac...  52.5 us
    ppermute x6, waiting for transfers between devices, shift_x(): lax.ppermute(a, 'col', [(seat(*p), seat(p[0], p[1] + s, p[2])) for p in s...  52.1 us
    ppermute x12, waiting for transfers between devices, shift_y(): return lax.ppermute(a, 'mem', [(i, (i + s) % y_n) for i in range(y_n)])  25 us
    ppermute x12, starting transfers between devices, shift_y(): return lax.ppermute(a, 'mem', [(i, (i + s) % y_n) for i in range(y_n)])  15.5 us
    all_to_all x2, starting transfers between devices, on_device(): arrived.append(lax.all_to_all(piece, 'col', 0, 0))  13.4 us
    ppermute x6, waiting for transfers between devices, shift_z(): lax.ppermute(a, 'col', [(seat(*p), seat(p[0] + s, p[1], p[2])) for p in s...  12.5 us
    ppermute x6, starting transfers between devices, shift_x(): lax.ppermute(a, 'col', [(seat(*p), seat(p[0], p[1] + s, p[2])) for p in s...  9.19 us
    ppermute x6, starting transfers between devices, shift_z(): lax.ppermute(a, 'col', [(seat(*p), seat(p[0] + s, p[1], p[2])) for p in s...  8.82 us
  transfers between devices with their start and end apart: 30, of which 17 were waited for; matrix products, arithmetic and copies ran while one was open for 5% of the time, Pallas kernels for 25%

profile of v1, /device:TPU:0, one launch (start us, length us, event | category | flops | bytes accessed | tf_op | source)
XLA Modules:
  0.0 212.1 jit_solution(17509563923623311455)
XLA Ops:
  0.0 4.8 %slice.89 = bf16[32,2,2,128,128]{4,3,2,1,0:T(8,128)(2,1)} slice(bf16[32,2,3,128,128]{4,3,2,1,0:T(8,128)(2,1)} %bitcast.100), slice={[0:32], [0:2], [0:2], [0:128], [0:128]} | slice | bytes 8388608 | tf_op jit(solution)/shard_map/slice | solution.py:145
  4.8 8.5 %all-to-all-start = ((bf16[32,2,2,128,128]{4,3,2,1,0:T(8,128)(2,1)}), bf16[32,2,2,128,128]{4,3,2,1,0:T(8,128)(2,1)}, u32[]{:S(2)}, u32[]{:S(2)}) async-start(bf16[32,2,2,128,128]{4,3,2,1,0:T(8,128)(2,1)} %slice.89), calls=%async_computation | async-start | bytes 8388608 | tf_op jit(solution)/shard_map/all_to_all | solution.py:148
  13.4 3.0 %collective-permute-start.2 = (bf16[3,32,128]{2,1,0:T(8,128)(2,1)S(1)}, bf16[3,32,128]{2,1,0:T(8,128)(2,1)S(1)}, u32[]{:S(2)}, u32[]{:S(2)}) collective-permute-start(bf16[3,32,128]{2,1,0:T(8,128)(2,1)S(1)} %copy-done.10), channel_id=1, source_target_pairs={{0,6},{1,7},{2,0},{3,1},{4,2},{5,3},{6,4},{7,5},{8,14},{9,15},{10,... | collective-permute-start | bytes 73736 | tf_op jit(solution)/shard_map/ppermute | solution.py:133
  18.1 46.0 %collective-permute-done.2 = bf16[3,32,128]{2,1,0:T(8,128)(2,1)S(1)} collective-permute-done((bf16[3,32,128]{2,1,0:T(8,128)(2,1)S(1)}, bf16[3,32,128]{2,1,0:T(8,128)(2,1)S(1)}, u32[]{:S(2)}, u32[]{:S(2)}) %collective-permute-start.2) | collective-permute-done | bytes 24608 | tf_op jit(solution)/shard_map/ppermute | solution.py:133
  66.0 3.2 %collective-permute-start.5 = (bf16[4,3,32,128]{3,2,1,0:T(8,128)(2,1)S(1)}, bf16[4,3,32,128]{3,2,1,0:T(8,128)(2,1)S(1)}, u32[]{:S(2)}, u32[]{:S(2)}) collective-permute-start(bf16[4,3,32,128]{3,2,1,0:T(8,128)(2,1)S(1)} %get-tuple-element.39), channel_id=1, source_target_pairs={{0,24},{1,25},{2,26},{3,27},{4,28},{5,29},{6,30},{7,31},{8,0},{9,1... | collective-permute-start | bytes 294920 | tf_op jit(solution)/shard_map/ppermute | solution.py:130
  70.1 2.6 %collective-permute-done.5 = bf16[4,3,32,128]{3,2,1,0:T(8,128)(2,1)S(1)} collective-permute-done((bf16[4,3,32,128]{3,2,1,0:T(8,128)(2,1)S(1)}, bf16[4,3,32,128]{3,2,1,0:T(8,128)(2,1)S(1)}, u32[]{:S(2)}, u32[]{:S(2)}) %collective-permute-start.5) | collective-permute-done | bytes 98336 | tf_op jit(solution)/shard_map/ppermute | solution.py:130
  72.7 2.7 %collective-permute-done.4 = bf16[4,3,32,128]{3,2,1,0:T(8,128)(2,1)S(1)} collective-permute-done((bf16[4,3,32,128]{3,2,1,0:T(8,128)(2,1)S(1)}, bf16[4,3,32,128]{3,2,1,0:T(8,128)(2,1)S(1)}, u32[]{:S(2)}, u32[]{:S(2)}) %collective-permute-start.4) | collective-permute-done | bytes 98336 | tf_op jit(solution)/shard_map/ppermute | solution.py:130
  76.4 3.1 %collective-permute-start.8 = (bf16[4,4,3,32,128]{4,3,2,1,0:T(8,128)(2,1)S(1)}, bf16[4,4,3,32,128]{4,3,2,1,0:T(8,128)(2,1)S(1)}, u32[]{:S(2)}, u32[]{:S(2)}) collective-permute-start(bf16[4,4,3,32,128]{4,3,2,1,0:T(8,128)(2,1)S(1)} %get-tuple-element.34), channel_id=1, source_target_pairs={{0,96},{32,0},{64,32},{96,64},{1,97},{33,1},{65,33},{97,65},{2,98}... | collective-permute-start | bytes 1179656 | tf_op jit(solution)/shard_map/ppermute | solution.py:127
  81.1 12.9 %collective-permute-done.8 = bf16[4,4,3,32,128]{4,3,2,1,0:T(8,128)(2,1)S(1)} collective-permute-done((bf16[4,4,3,32,128]{4,3,2,1,0:T(8,128)(2,1)S(1)}, bf16[4,4,3,32,128]{4,3,2,1,0:T(8,128)(2,1)S(1)}, u32[]{:S(2)}, u32[]{:S(2)}) %collective-permute-start.8) | collective-permute-done | bytes 393248 | tf_op jit(solution)/shard_map/ppermute | solution.py:127
  94.0 3.7 %collective-permute-done.6 = bf16[4,4,3,32,128]{4,3,2,1,0:T(8,128)(2,1)S(1)} collective-permute-done((bf16[4,4,3,32,128]{4,3,2,1,0:T(8,128)(2,1)S(1)}, bf16[4,4,3,32,128]{4,3,2,1,0:T(8,128)(2,1)S(1)}, u32[]{:S(2)}, u32[]{:S(2)}) %collective-permute-start.6) | collective-permute-done | bytes 393248 | tf_op jit(solution)/shard_map/ppermute | solution.py:127
  98.0 3.2 %slice.88 = bf16[32,2,1,128,128]{4,3,2,1,0:T(8,128)(2,1)} slice(bf16[32,2,3,128,128]{4,3,2,1,0:T(8,128)(2,1)} %bitcast.101), slice={[0:32], [0:2], [2:3], [0:128], [0:128]} | slice | bytes 4194304 | tf_op jit(solution)/shard_map/slice | solution.py:145
  101.2 4.9 %all-to-all-start.1 = ((bf16[32,2,1,128,128]{4,3,2,1,0:T(8,128)(2,1)}), bf16[32,2,1,128,128]{4,3,2,1,0:T(8,128)(2,1)}, u32[]{:S(2)}, u32[]{:S(2)}) async-start(bf16[32,2,1,128,128]{4,3,2,1,0:T(8,128)(2,1)} %slice.88), calls=%async_computation.1 | async-start | bytes 4194304 | tf_op jit(solution)/shard_map/all_to_all | solution.py:148
  111.5 17.4 %members_1.1 = (bf16[4,4,4,32,128]{4,3,2,1,0:T(8,128)(2,1)S(1)}, bf16[4,4,4,32,128]{4,3,2,1,0:T(8,128)(2,1)S(1)}) custom-call(s32[4]{0:T(128)S(1)} %pad_add_fusion.where_ref, s32[32,8]{1,0:T(8,128)S(1)} %copy.8.cols_ref, bf16[32,2,2,128,128]{4,3,2,1,0:T(8,128)(2,1)} %all-to-all-done.ens_ref, bf16[4,4,4,3,32,128]{5,4,3,2,1,0:T(8,128)(2,1)S(1)} %pad_maximum_fusion.mine_ref, ...), custom_call_target="tpu_custom_call" | custom-call | tf_op jit(solution)/shard_map/members_1/pallas_call | solution.py:180
  129.3 18.2 %members_0.1 = (bf16[4,4,4,32,128]{4,3,2,1,0:T(8,128)(2,1)S(1)}, bf16[4,4,4,32,128]{4,3,2,1,0:T(8,128)(2,1)}) custom-call(s32[4]{0:T(128)S(1)} %pad_add_fusion.where_ref, s32[32,8]{1,0:T(8,128)S(1)} %copy.8.cols_ref, bf16[32,2,2,128,128]{4,3,2,1,0:T(8,128)(2,1)} %all-to-all-done.ens_ref, bf16[4,4,4,3,32,128]{5,4,3,2,1,0:T(8,128)(2,1)S(1)} %pad_maximum_fusion.mine_ref, ...), custom_call_target="tpu_custom_call" | custom-call | tf_op jit(solution)/shard_map/members_0/pallas_call | solution.py:180
  154.8 16.9 %members_2.1 = (bf16[4,4,4,32,128]{4,3,2,1,0:T(8,128)(2,1)S(1)}, bf16[4,4,4,32,128]{4,3,2,1,0:T(8,128)(2,1)S(1)}) custom-call(s32[4]{0:T(128)S(1)} %copy-done.8, s32[32,8]{1,0:T(8,128)S(1)} %copy.8.cols_ref, bf16[32,2,1,128,128]{4,3,2,1,0:T(8,128)(2,1)} %all-to-all-done.1.ens_ref, bf16[4,4,4,3,32,128]{5,4,3,2,1,0:T(8,128)(2,1)S(1)} %pad_maximum_fusion.mine_ref, ...), custom_call_target="tpu_custom_call" | custom-call | tf_op jit(solution)/shard_map/members_2/pallas_call | solution.py:180
  173.1 2.7 %collective-permute-start.13 = (bf16[4,4,32,128]{3,2,1,0:T(8,128)(2,1)S(1)}, bf16[4,4,32,128]{3,2,1,0:T(8,128)(2,1)S(1)}, u32[]{:S(2)}, u32[]{:S(2)}) collective-permute-start(bf16[4,4,32,128]{3,2,1,0:T(8,128)(2,1)S(1)} %get-tuple-element.22), channel_id=1, source_target_pairs={{0,96},{32,0},{64,32},{96,64},{1,97},{33,1},{65,33},{97,65},{2,98}... | collective-permute-start | bytes 393224 | tf_op jit(solution)/shard_map/ppermute | solution.py:127
  180.0 2.2 %collective-permute-start.21 = (bf16[4,4,32,128]{3,2,1,0:T(8,128)(2,1)S(1)}, bf16[4,4,32,128]{3,2,1,0:T(8,128)(2,1)S(1)}, u32[]{:S(2)}, u32[]{:S(2)}) collective-permute-start(bf16[4,4,32,128]{3,2,1,0:T(8,128)(2,1)S(1)} %get-tuple-element.28), channel_id=1, source_target_pairs={{0,96},{32,0},{64,32},{96,64},{1,97},{33,1},{65,33},{97,65},{2,98}... | collective-permute-start | bytes 393224 | tf_op jit(solution)/shard_map/ppermute | solution.py:127
  185.8 2.1 %collective-permute-done.21 = bf16[4,4,32,128]{3,2,1,0:T(8,128)(2,1)S(1)} collective-permute-done((bf16[4,4,32,128]{3,2,1,0:T(8,128)(2,1)S(1)}, bf16[4,4,32,128]{3,2,1,0:T(8,128)(2,1)S(1)}, u32[]{:S(2)}, u32[]{:S(2)}) %collective-permute-start.21) | collective-permute-done | bytes 131104 | tf_op jit(solution)/shard_map/ppermute | solution.py:127
  187.9 2.2 %collective-permute-done.20 = bf16[4,4,32,128]{3,2,1,0:T(8,128)(2,1)S(1)} collective-permute-done((bf16[4,4,32,128]{3,2,1,0:T(8,128)(2,1)S(1)}, bf16[4,4,32,128]{3,2,1,0:T(8,128)(2,1)S(1)}, u32[]{:S(2)}, u32[]{:S(2)}) %collective-permute-start.20) | collective-permute-done | bytes 131104 | tf_op jit(solution)/shard_map/ppermute | solution.py:127
  191.7 3.0 %collective-permute-start.24 = (bf16[4,3,32,128]{3,2,0,1:T(8,128)(2,1)S(1)}, bf16[4,3,32,128]{3,2,0,1:T(8,128)(2,1)S(1)}, u32[]{:S(2)}, u32[]{:S(2)}) collective-permute-start(bf16[4,3,32,128]{3,2,0,1:T(8,128)(2,1)S(1)} %get-tuple-element.31), channel_id=1, source_target_pairs={{0,24},{1,25},{2,26},{3,27},{4,28},{5,29},{6,30},{7,31},{8,0},{9,1... | collective-permute-start | bytes 294920 | tf_op jit(solution)/shard_map/ppermute | solution.py:130
  196.4 2.6 %collective-permute-done.24 = bf16[4,3,32,128]{3,2,0,1:T(8,128)(2,1)S(1)} collective-permute-done((bf16[4,3,32,128]{3,2,0,1:T(8,128)(2,1)S(1)}, bf16[4,3,32,128]{3,2,0,1:T(8,128)(2,1)S(1)}, u32[]{:S(2)}, u32[]{:S(2)}) %collective-permute-start.24) | collective-permute-done | bytes 98336 | tf_op jit(solution)/shard_map/ppermute | solution.py:130
  199.1 2.6 %collective-permute-done.23 = bf16[4,3,32,128]{3,2,0,1:T(8,128)(2,1)S(1)} collective-permute-done((bf16[4,3,32,128]{3,2,0,1:T(8,128)(2,1)S(1)}, bf16[4,3,32,128]{3,2,0,1:T(8,128)(2,1)S(1)}, u32[]{:S(2)}, u32[]{:S(2)}) %collective-permute-start.23) | collective-permute-done | bytes 98336 | tf_op jit(solution)/shard_map/ppermute | solution.py:130
  202.8 2.8 %collective-permute-start.27 = (bf16[3,32,128]{2,1,0:T(8,128)(2,1)S(1)}, bf16[3,32,128]{2,1,0:T(8,128)(2,1)S(1)}, u32[]{:S(2)}, u32[]{:S(2)}) collective-permute-start(bf16[3,32,128]{2,1,0:T(8,128)(2,1)S(1)} %get-tuple-element.36), channel_id=1, source_target_pairs={{0,6},{1,7},{2,0},{3,1},{4,2},{5,3},{6,4},{7,5},{8,14},{9,15},{10,... | collective-permute-start | bytes 73736 | tf_op jit(solution)/shard_map/ppermute | solution.py:133
  207.3 3.6 %collective-permute-done.26 = bf16[3,32,128]{2,1,0:T(8,128)(2,1)S(1)} collective-permute-done((bf16[3,32,128]{2,1,0:T(8,128)(2,1)S(1)}, bf16[3,32,128]{2,1,0:T(8,128)(2,1)S(1)}, u32[]{:S(2)}, u32[]{:S(2)}) %collective-permute-start.26) | collective-permute-done | bytes 24608 | tf_op jit(solution)/shard_map/ppermute | solution.py:133
  (91 shorter events, 36.9 us)
Async XLA Ops:
  4.8 96.4 %all-to-all-start = ((bf16[32,2,2,128,128]{4,3,2,1,0:T(8,128)(2,1)}), bf16[32,2,2,128,128]{4,3,2,1,0:T(8,128)(2,1)}, u32[]{:S(2)}, u32[]{:S(2)}) async-start(bf16[32,2,2,128,128]{4,3,2,1,0:T(8,128)(2,1)} %slice.89), calls=%async_computation | async-start | bytes 8388608 | tf_op jit(solution)/shard_map/all_to_all | solution.py:148
  13.4 50.7 %collective-permute-start.2 = (bf16[3,32,128]{2,1,0:T(8,128)(2,1)S(1)}, bf16[3,32,128]{2,1,0:T(8,128)(2,1)S(1)}, u32[]{:S(2)}, u32[]{:S(2)}) collective-permute-start(bf16[3,32,128]{2,1,0:T(8,128)(2,1)S(1)} %copy-done.10), channel_id=1, source_target_pairs={{0,6},{1,7},{2,0},{3,1},{4,2},{5,3},{6,4},{7,5},{8,14},{9,15},{10,... | collective-permute-start | bytes 73736 | tf_op jit(solution)/shard_map/ppermute | solution.py:133
  16.3 49.6 %collective-permute-start.1 = (bf16[3,32,128]{2,1,0:T(8,128)(2,1)S(1)}, bf16[3,32,128]{2,1,0:T(8,128)(2,1)S(1)}, u32[]{:S(2)}, u32[]{:S(2)}) collective-permute-start(bf16[3,32,128]{2,1,0:T(8,128)(2,1)S(1)} %copy-done.10), channel_id=1, source_target_pairs={{0,4},{1,5},{2,6},{3,7},{4,0},{5,1},{6,2},{7,3},{8,12},{9,13},{10,... | collective-permute-start | bytes 73736 | tf_op jit(solution)/shard_map/ppermute | solution.py:133
  17.2 48.8 %collective-permute-start = (bf16[3,32,128]{2,1,0:T(8,128)(2,1)S(1)}, bf16[3,32,128]{2,1,0:T(8,128)(2,1)S(1)}, u32[]{:S(2)}, u32[]{:S(2)}) collective-permute-start(bf16[3,32,128]{2,1,0:T(8,128)(2,1)S(1)} %copy-done.10), channel_id=1, source_target_pairs={{0,2},{1,3},{2,4},{3,5},{4,6},{5,7},{6,0},{7,1},{8,10},{9,11},{10,... | collective-permute-start | bytes 73736 | tf_op jit(solution)/shard_map/ppermute | solution.py:133
  76.4 17.6 %collective-permute-start.8 = (bf16[4,4,3,32,128]{4,3,2,1,0:T(8,128)(2,1)S(1)}, bf16[4,4,3,32,128]{4,3,2,1,0:T(8,128)(2,1)S(1)}, u32[]{:S(2)}, u32[]{:S(2)}) collective-permute-start(bf16[4,4,3,32,128]{4,3,2,1,0:T(8,128)(2,1)S(1)} %get-tuple-element.34), channel_id=1, source_target_pairs={{0,96},{32,0},{64,32},{96,64},{1,97},{33,1},{65,33},{97,65},{2,98}... | collective-permute-start | bytes 1179656 | tf_op jit(solution)/shard_map/ppermute | solution.py:127
  79.5 14.5 %collective-permute-start.7 = (bf16[4,4,3,32,128]{4,3,2,1,0:T(8,128)(2,1)S(1)}, bf16[4,4,3,32,128]{4,3,2,1,0:T(8,128)(2,1)S(1)}, u32[]{:S(2)}, u32[]{:S(2)}) collective-permute-start(bf16[4,4,3,32,128]{4,3,2,1,0:T(8,128)(2,1)S(1)} %get-tuple-element.34), channel_id=1, source_target_pairs={{0,64},{32,96},{64,0},{96,32},{1,65},{33,97},{65,1},{97,33},{2,66}... | collective-permute-start | bytes 1179656 | tf_op jit(solution)/shard_map/ppermute | solution.py:127
  80.1 17.6 %collective-permute-start.6 = (bf16[4,4,3,32,128]{4,3,2,1,0:T(8,128)(2,1)S(1)}, bf16[4,4,3,32,128]{4,3,2,1,0:T(8,128)(2,1)S(1)}, u32[]{:S(2)}, u32[]{:S(2)}) collective-permute-start(bf16[4,4,3,32,128]{4,3,2,1,0:T(8,128)(2,1)S(1)} %get-tuple-element.34), channel_id=1, source_target_pairs={{0,32},{32,64},{64,96},{96,0},{1,33},{33,65},{65,97},{97,1},{2,34}... | collective-permute-start | bytes 1179656 | tf_op jit(solution)/shard_map/ppermute | solution.py:127
  97.9 11.8 %collective-permute-start.9 = (bf16[4,4,4,3,32,128]{5,4,3,2,1,0:T(8,128)(2,1)S(1)}, bf16[4,4,4,3,32,128]{5,4,3,2,1,0:T(8,128)(2,1)S(1)}, u32[]{:S(2)}, u32[]{:S(2)}) collective-permute-start(bf16[4,4,4,3,32,128]{5,4,3,2,1,0:T(8,128)(2,1)S(1)} %pad_maximum_fusion.mine_ref), channel_id=1, source_target_pairs={{0,1},{1,0},{2,3},{3,2},{4,5},{5,4},{6,7},{7,6},{8,9},{9,8},{10,11... | collective-permute-start | bytes 4718600 | tf_op jit(solution)/shard_map/ppermute | solution.py:136
  101.2 51.2 %all-to-all-start.1 = ((bf16[32,2,1,128,128]{4,3,2,1,0:T(8,128)(2,1)}), bf16[32,2,1,128,128]{4,3,2,1,0:T(8,128)(2,1)}, u32[]{:S(2)}, u32[]{:S(2)}) async-start(bf16[32,2,1,128,128]{4,3,2,1,0:T(8,128)(2,1)} %slice.88), calls=%async_computation.1 | async-start | bytes 4194304 | tf_op jit(solution)/shard_map/all_to_all | solution.py:148
  128.9 19.7 %collective-permute-start.14 = (bf16[4,4,4,32,128]{4,3,2,1,0:T(8,128)(2,1)S(1)}, bf16[4,4,4,32,128]{4,3,2,1,0:T(8,128)(2,1)S(1)}, u32[]{:S(2)}, u32[]{:S(2)}) collective-permute-start(bf16[4,4,4,32,128]{4,3,2,1,0:T(8,128)(2,1)S(1)} %get-tuple-element.17), channel_id=1, source_target_pairs={{0,1},{1,0},{2,3},{3,2},{4,5},{5,4},{6,7},{7,6},{8,9},{9,8},{10,11... | collective-permute-start | bytes 1572872 | tf_op jit(solution)/shard_map/ppermute | solution.py:136
  148.3 23.5 %collective-permute-start.10 = (bf16[4,4,4,32,128]{4,3,2,1,0:T(8,128)(2,1)}, bf16[4,4,4,32,128]{4,3,2,1,0:T(8,128)(2,1)}, u32[]{:S(2)}, u32[]{:S(2)}) collective-permute-start(bf16[4,4,4,32,128]{4,3,2,1,0:T(8,128)(2,1)} %get-tuple-element.15), channel_id=1, source_target_pairs={{0,1},{1,0},{2,3},{3,2},{4,5},{5,4},{6,7},{7,6},{8,9},{9,8},{10,11... | collective-permute-start | bytes 1572872 | tf_op jit(solution)/shard_map/ppermute | solution.py:136
  150.3 25.5 %collective-permute-start.17 = (bf16[4,4,32,128]{3,2,1,0:T(8,128)(2,1)}, bf16[4,4,32,128]{3,2,1,0:T(8,128)(2,1)}, u32[]{:S(2)}, u32[]{:S(2)}) collective-permute-start(bf16[4,4,32,128]{3,2,1,0:T(8,128)(2,1)} %get-tuple-element.25), channel_id=1, source_target_pairs={{0,96},{32,0},{64,32},{96,64},{1,97},{33,1},{65,33},{97,65},{2,98}... | collective-permute-start | bytes 393224 | tf_op jit(solution)/shard_map/ppermute | solution.py:127
  150.9 26.4 %collective-permute-start.16 = (bf16[4,4,32,128]{3,2,1,0:T(8,128)(2,1)}, bf16[4,4,32,128]{3,2,1,0:T(8,128)(2,1)}, u32[]{:S(2)}, u32[]{:S(2)}) collective-permute-start(bf16[4,4,32,128]{3,2,1,0:T(8,128)(2,1)} %get-tuple-element.26), channel_id=1, source_target_pairs={{0,64},{32,96},{64,0},{96,32},{1,65},{33,97},{65,1},{97,33},{2,66}... | collective-permute-start | bytes 393224 | tf_op jit(solution)/shard_map/ppermute | solution.py:127
  151.6 27.1 %collective-permute-start.15 = (bf16[4,4,32,128]{3,2,1,0:T(8,128)(2,1)}, bf16[4,4,32,128]{3,2,1,0:T(8,128)(2,1)}, u32[]{:S(2)}, u32[]{:S(2)}) collective-permute-start(bf16[4,4,32,128]{3,2,1,0:T(8,128)(2,1)} %get-tuple-element.24), channel_id=1, source_target_pairs={{0,32},{32,64},{64,96},{96,0},{1,33},{33,65},{65,97},{97,1},{2,34}... | collective-permute-start | bytes 393224 | tf_op jit(solution)/shard_map/ppermute | solution.py:127
  171.7 8.1 %collective-permute-start.18 = (bf16[4,4,4,32,128]{4,3,2,1,0:T(8,128)(2,1)S(1)}, bf16[4,4,4,32,128]{4,3,2,1,0:T(8,128)(2,1)S(1)}, u32[]{:S(2)}, u32[]{:S(2)}) collective-permute-start(bf16[4,4,4,32,128]{4,3,2,1,0:T(8,128)(2,1)S(1)} %get-tuple-element.20), channel_id=1, source_target_pairs={{0,1},{1,0},{2,3},{3,2},{4,5},{5,4},{6,7},{7,6},{8,9},{9,8},{10,11... | collective-permute-start | bytes 1572872 | tf_op jit(solution)/shard_map/ppermute | solution.py:136
  173.1 9.9 %collective-permute-start.13 = (bf16[4,4,32,128]{3,2,1,0:T(8,128)(2,1)S(1)}, bf16[4,4,32,128]{3,2,1,0:T(8,128)(2,1)S(1)}, u32[]{:S(2)}, u32[]{:S(2)}) collective-permute-start(bf16[4,4,32,128]{3,2,1,0:T(8,128)(2,1)S(1)} %get-tuple-element.22), channel_id=1, source_target_pairs={{0,96},{32,0},{64,32},{96,64},{1,97},{33,1},{65,33},{97,65},{2,98}... | collective-permute-start | bytes 393224 | tf_op jit(solution)/shard_map/ppermute | solution.py:127
  175.8 7.9 %collective-permute-start.12 = (bf16[4,4,32,128]{3,2,1,0:T(8,128)(2,1)S(1)}, bf16[4,4,32,128]{3,2,1,0:T(8,128)(2,1)S(1)}, u32[]{:S(2)}, u32[]{:S(2)}) collective-permute-start(bf16[4,4,32,128]{3,2,1,0:T(8,128)(2,1)S(1)} %get-tuple-element.23), channel_id=1, source_target_pairs={{0,64},{32,96},{64,0},{96,32},{1,65},{33,97},{65,1},{97,33},{2,66}... | collective-permute-start | bytes 393224 | tf_op jit(solution)/shard_map/ppermute | solution.py:127
  177.3 8.4 %collective-permute-start.11 = (bf16[4,4,32,128]{3,2,1,0:T(8,128)(2,1)S(1)}, bf16[4,4,32,128]{3,2,1,0:T(8,128)(2,1)S(1)}, u32[]{:S(2)}, u32[]{:S(2)}) collective-permute-start(bf16[4,4,32,128]{3,2,1,0:T(8,128)(2,1)S(1)} %get-tuple-element.21), channel_id=1, source_target_pairs={{0,32},{32,64},{64,96},{96,0},{1,33},{33,65},{65,97},{97,1},{2,34}... | collective-permute-start | bytes 393224 | tf_op jit(solution)/shard_map/ppermute | solution.py:127
  180.0 7.8 %collective-permute-start.21 = (bf16[4,4,32,128]{3,2,1,0:T(8,128)(2,1)S(1)}, bf16[4,4,32,128]{3,2,1,0:T(8,128)(2,1)S(1)}, u32[]{:S(2)}, u32[]{:S(2)}) collective-permute-start(bf16[4,4,32,128]{3,2,1,0:T(8,128)(2,1)S(1)} %get-tuple-element.28), channel_id=1, source_target_pairs={{0,96},{32,0},{64,32},{96,64},{1,97},{33,1},{65,33},{97,65},{2,98}... | collective-permute-start | bytes 393224 | tf_op jit(solution)/shard_map/ppermute | solution.py:127
  182.2 7.9 %collective-permute-start.20 = (bf16[4,4,32,128]{3,2,1,0:T(8,128)(2,1)S(1)}, bf16[4,4,32,128]{3,2,1,0:T(8,128)(2,1)S(1)}, u32[]{:S(2)}, u32[]{:S(2)}) collective-permute-start(bf16[4,4,32,128]{3,2,1,0:T(8,128)(2,1)S(1)} %get-tuple-element.29), channel_id=1, source_target_pairs={{0,64},{32,96},{64,0},{96,32},{1,65},{33,97},{65,1},{97,33},{2,66}... | collective-permute-start | bytes 393224 | tf_op jit(solution)/shard_map/ppermute | solution.py:127
  183.0 8.6 %collective-permute-start.19 = (bf16[4,4,32,128]{3,2,1,0:T(8,128)(2,1)S(1)}, bf16[4,4,32,128]{3,2,1,0:T(8,128)(2,1)S(1)}, u32[]{:S(2)}, u32[]{:S(2)}) collective-permute-start(bf16[4,4,32,128]{3,2,1,0:T(8,128)(2,1)S(1)} %get-tuple-element.27), channel_id=1, source_target_pairs={{0,32},{32,64},{64,96},{96,0},{1,33},{33,65},{65,97},{97,1},{2,34}... | collective-permute-start | bytes 393224 | tf_op jit(solution)/shard_map/ppermute | solution.py:127
  191.7 7.3 %collective-permute-start.24 = (bf16[4,3,32,128]{3,2,0,1:T(8,128)(2,1)S(1)}, bf16[4,3,32,128]{3,2,0,1:T(8,128)(2,1)S(1)}, u32[]{:S(2)}, u32[]{:S(2)}) collective-permute-start(bf16[4,3,32,128]{3,2,0,1:T(8,128)(2,1)S(1)} %get-tuple-element.31), channel_id=1, source_target_pairs={{0,24},{1,25},{2,26},{3,27},{4,28},{5,29},{6,30},{7,31},{8,0},{9,1... | collective-permute-start | bytes 294920 | tf_op jit(solution)/shard_map/ppermute | solution.py:130
  194.8 6.9 %collective-permute-start.23 = (bf16[4,3,32,128]{3,2,0,1:T(8,128)(2,1)S(1)}, bf16[4,3,32,128]{3,2,0,1:T(8,128)(2,1)S(1)}, u32[]{:S(2)}, u32[]{:S(2)}) collective-permute-start(bf16[4,3,32,128]{3,2,0,1:T(8,128)(2,1)S(1)} %get-tuple-element.32), channel_id=1, source_target_pairs={{0,16},{1,17},{2,18},{3,19},{4,20},{5,21},{6,22},{7,23},{8,24},{9,... | collective-permute-start | bytes 294920 | tf_op jit(solution)/shard_map/ppermute | solution.py:130
  195.5 7.2 %collective-permute-start.22 = (bf16[4,3,32,128]{3,2,0,1:T(8,128)(2,1)S(1)}, bf16[4,3,32,128]{3,2,0,1:T(8,128)(2,1)S(1)}, u32[]{:S(2)}, u32[]{:S(2)}) collective-permute-start(bf16[4,3,32,128]{3,2,0,1:T(8,128)(2,1)S(1)} %get-tuple-element.30), channel_id=1, source_target_pairs={{0,8},{1,9},{2,10},{3,11},{4,12},{5,13},{6,14},{7,15},{8,16},{9,17... | collective-permute-start | bytes 294920 | tf_op jit(solution)/shard_map/ppermute | solution.py:130
  (19 other events, 101.0 us)

commit v2 on v1

--- a/solution.py
+++ b/solution.py
@@ -10,6 +10,7 @@
 BF = jnp.bfloat16
 F32 = jnp.float32
 CORES = 2
+FLOOR = 2
 
 
 def member_kernel(
@@ -23,7 +24,6 @@
     y_n, z_n, x_n = mine_ref.shape[0], mine_ref.shape[1], mine_ref.shape[2]
     part_l = mine_ref.shape[4]
     slots = cols_ref.shape[1]
-    pairs = slots // 2
     my_y, my_z, my_x, my_c = where_ref[0], where_ref[1], where_ref[2], where_ref[3]
     n_copies = sems.shape[0]
     per_copy = n_blocks // n_copies
@@ -54,7 +54,9 @@
         weighted = jnp.concatenate(halves, axis=1)
         lift = jnp.dot(vt_ref[var], weighted, preferred_element_type=F32).astype(BF)
         for m in range(members):
-            lifted[block, m * levels:(m + 1) * levels, :] = lift[:, m * width:(m + 1) * width]
+            lifted[block, :, m * levels:(m + 1) * levels] = jnp.swapaxes(
+                lift[:, m * width:(m + 1) * width], 0, 1
+            )
 
     def lift_step(step, carry):
         off_z, off_x, base = seat_of(step)
@@ -64,28 +66,26 @@
         lift_block(other_ref, base + 1 - my_c, in_z, in_x)
         return carry
 
-    lax.fori_loop(0, n_blocks // CORES, lift_step, 0)
+    lax.fori_loop(0, n_blocks // CORES, lift_step, 0, unroll=2)
     for piece in range(n_copies):
         tile_copy(piece).wait()
 
     def spread_block(target_ref, block, off_z, off_x):
-        acc = None
-        for pair in range(pairs):
-            first = lifted[cols_ref[block, 2 * pair]]
-            second = lifted[cols_ref[block, 2 * pair + 1]]
-            both = jnp.concatenate([first, second], axis=1)
-            if pair > 0:
-                both = both * mask_ref[pair - 1]
-            term = jnp.dot(
-                both, tile_buf[block, 2 * pair * width:2 * (pair + 1) * width, :],
-                preferred_element_type=F32,
-            )
-            acc = term if acc is None else acc + term
-        spread = acc.astype(BF)
+        parts = []
+        for slot in range(slots):
+            picked = lifted[cols_ref[block, slot]]
+            if slot >= FLOOR:
+                picked = picked * mask_ref[slot - FLOOR]
+            parts.append(picked)
+        spread = jnp.dot(
+            tile_buf[block], jnp.concatenate(parts, axis=0), preferred_element_type=F32
+        ).astype(BF)
         beside = jnp.concatenate(
-            [spread[m * levels:(m + 1) * levels, :] for m in range(members)], axis=1
+            [spread[:, m * levels:(m + 1) * levels] for m in range(members)], axis=0
         )
-        lowered = jnp.dot(vn_ref[var], beside, preferred_element_type=F32)
+        lowered = lax.dot_general(
+            vn_ref[var], beside, (((1,), (1,)), ((), ())), preferred_element_type=F32
+        )
         total = None
         for m in range(members):
             term = ens_ref[block, m, slot_of_var].astype(F32) * lowered[:, m * width:(m + 1) * width]
@@ -101,7 +101,7 @@
         spread_block(far_ref, base + 1 - my_c, off_z, off_x)
         return carry
 
-    lax.fori_loop(0, n_blocks // CORES, spread_step, 0)
+    lax.fori_loop(0, n_blocks // CORES, spread_step, 0, unroll=2)
 
 
 def on_device(
@@ -140,29 +140,28 @@
 
     by_member = ensemble.reshape(columns, members, n_var, levels, width)
     groups = ((0, 1), (2,))
-    arrived, where_var = [], {}
-    for index, group in enumerate(groups):
-        piece = by_member[:, :, group[0]:group[-1] + 1]
-        if arrived:
-            piece, arrived[-1] = lax.optimization_barrier((piece, arrived[-1]))
-        arrived.append(lax.all_to_all(piece, "col", 0, 0))
-        for place, var in enumerate(group):
-            where_var[var] = (index, place)
+    pieces = [by_member[:, :, group[0]:group[-1] + 1] for group in groups]
+    where_var = {
+        var: (index, place) for index, group in enumerate(groups) for place, var in enumerate(group)
+    }
 
     mine = collect(increment, shift_x, x_n)
     mine = collect(mine, shift_z, z_n)
+    pieces[0], mine = lax.optimization_barrier((pieces[0], mine))
+    arrived = [lax.all_to_all(pieces[0], "col", 0, 0)]
+    mine, pieces[1], tiles = lax.optimization_barrier((mine, pieces[1], tiles))
+    turned_tiles = jnp.transpose(tiles, (0, 3, 1, 2)).reshape(columns, width, slots * width)
     mine = collect(mine, shift_y, y_n)
+    mine, turned_tiles = lax.optimization_barrier((mine, turned_tiles))
     other = swap(mine)
+    pieces[1], arrived[0] = lax.optimization_barrier((pieces[1], arrived[0]))
+    arrived.append(lax.all_to_all(pieces[1], "col", 0, 0))
 
     vert_t = jnp.swapaxes(vert_root, 1, 2)
     active = (
-        jnp.arange(2, slots, dtype=jnp.int32)[:, None] < level_reach[None, :]
-    ).astype(BF).reshape(slots // 2 - 1, 2, levels)
-    active = jnp.swapaxes(active, 1, 2)
-    mask = jnp.broadcast_to(
-        active[:, None, :, :, None], (slots // 2 - 1, members, levels, 2, width)
-    ).reshape(slots // 2 - 1, members * levels, 2 * width)
-    flat_tiles = tiles.reshape(columns, slots * width, width)
+        jnp.arange(FLOOR, slots, dtype=jnp.int32)[:, None] < level_reach[None, :]
+    ).astype(BF)
+    mask = jnp.tile(active, (1, members))[:, None, :]
 
     vmem = pl.BlockSpec(memory_space=pltpu.VMEM)
     smem = pl.BlockSpec(memory_space=pltpu.SMEM)
@@ -177,6 +176,8 @@
     held = []
     for var in range(n_var):
         index, place = where_var[var]
+        if index and place == 0:
+            arrived[index], *held = lax.optimization_barrier((arrived[index], *held))
         near, far = pl.pallas_call(
             functools.partial(member_kernel, var=var, slot_of_var=place),
             out_shape=(out, out),
@@ -184,13 +185,13 @@
                       pl.BlockSpec(memory_space=pl.ANY)],
             out_specs=(vmem, vmem),
             scratch_shapes=[
-                pltpu.VMEM(flat_tiles.shape, BF),
-                pltpu.VMEM((columns, members * levels, width), BF),
+                pltpu.VMEM(turned_tiles.shape, BF),
+                pltpu.VMEM((columns, width, members * levels), BF),
                 pltpu.SemaphoreType.DMA((4,)),
             ],
             compiler_params=pltpu.CompilerParams(vmem_limit_bytes=40 << 20),
             name=f"members_{var}",
-        )(where, tile_col, arrived[index], mine, other, vert_t, vert_root, mask, flat_tiles)
+        )(where, tile_col, arrived[index], mine, other, vert_t, vert_root, mask, turned_tiles)
         chip = add([near, swap(far)]).astype(BF)
         held.append(add([chip[0]] + [shift_y(chip[s], s) for s in range(1, y_n)]).astype(BF))
     held = jnp.stack(held, axis=2)

time: 213 us -> 187 us (0.88)
  waiting for transfers between devices: 89.6 us -> 68.5 us
  Pallas kernels: 52.5 us -> 48.1 us
  local copies, waits for them, and re-layouts: 18 us -> 20.5 us
  starting transfers between devices: 47.7 us -> 45.4 us
    ppermute x6, waiting for transfers between devices: 52.1 us -> 8.53 us  [shift_x(): lax.ppermute(a, 'col', [(seat(*p), seat(p[0], p[1] + s, p[2])) for p in s...]
    all_to_all x2, waiting for transfers between devices: 0.01 us -> 26.2 us  [the longest x1 26.2 us: on_device(): arrived = [lax.all_to_all(pieces[0], 'col', 0, 0)]]
    reshape x1, local copies, waits for them, and re-layouts: 1.24 us -> 11.9 us  [on_device(): jnp.transpose(tiles, (0, 3, 1, 2)).reshape(columns, width, slots * width)]
    unnamed x28 -> x10, local copies, waits for them, and re-layouts: 6.72 us -> 0.47 us
    ppermute x6, waiting for transfers between devices: 12.5 us -> 7.28 us  [shift_z(): lax.ppermute(a, 'col', [(seat(*p), seat(p[0] + s, p[1], p[2])) for p in s...]
    pallas_call x3, Pallas kernels: 52.5 us -> 48.1 us  [on_device(): pl.pallas_call(functools.partial(member_kernel, var=var, slot_of_var=plac...]
    all_to_all x2, starting transfers between devices: 13.4 us -> 9.65 us  [the longest x1 4.88 us: on_device(): arrived = [lax.all_to_all(pieces[0], 'col', 0, 0)]]
  transfers between devices with their start and end apart: 30 -> 30, of which waited for: 17 -> 21; matrix products, arithmetic and copies ran while one was open for 5% -> 12% of each run, Pallas kernels for 25% -> 17%
where the time goes in v2:
time: 187 us; the launch traced here: 186 us
  waiting for transfers between devices  68.5 us (37%)
  Pallas kernels  48.1 us (26%)
  starting transfers between devices  45.4 us (24%)
  local copies, waits for them, and re-layouts  20.5 us (11%)
  other arithmetic  3.22 us (2%)
    pallas_call x3, Pallas kernels, on_device(): pl.pallas_call(functools.partial(member_kernel, var=var, slot_of_var=plac...  48.1 us
    all_to_all x1, waiting for transfers between devices, on_device(): arrived = [lax.all_to_all(pieces[0], 'col', 0, 0)]  26.2 us
    ppermute x12, waiting for transfers between devices, shift_y(): return lax.ppermute(a, 'mem', [(i, (i + s) % y_n) for i in range(y_n)])  24.6 us
    ppermute x12, starting transfers between devices, shift_y(): return lax.ppermute(a, 'mem', [(i, (i + s) % y_n) for i in range(y_n)])  15.4 us
    reshape x1, local copies, waits for them, and re-layouts, on_device(): jnp.transpose(tiles, (0, 3, 1, 2)).reshape(columns, width, slots * width)  11.9 us
    ppermute x6, starting transfers between devices, shift_z(): lax.ppermute(a, 'col', [(seat(*p), seat(p[0] + s, p[1], p[2])) for p in s...  10.1 us
    ppermute x6, starting transfers between devices, shift_x(): lax.ppermute(a, 'col', [(seat(*p), seat(p[0], p[1] + s, p[2])) for p in s...  9.04 us
    ppermute x6, waiting for transfers between devices, shift_x(): lax.ppermute(a, 'col', [(seat(*p), seat(p[0], p[1] + s, p[2])) for p in s...  8.53 us
  transfers between devices with their start and end apart: 30, of which 21 were waited for; matrix products, arithmetic and copies ran while one was open for 12% of the time, Pallas kernels for 17%

profile of v2, /device:TPU:0, one launch (start us, length us, event | category | flops | bytes accessed | tf_op | source)
XLA Modules:
  0.0 185.9 jit_solution(17923009837435533119)
XLA Ops:
  0.0 2.9 %collective-permute-start.2 = (bf16[3,32,128]{2,1,0:T(8,128)(2,1)}, bf16[3,32,128]{2,1,0:T(8,128)(2,1)S(1)}, u32[]{:S(2)}, u32[]{:S(2)}) collective-permute-start(bf16[3,32,128]{2,1,0:T(8,128)(2,1)} %param.7), channel_id=1, source_target_pairs={{0,6},{1,7},{2,0},{3,1},{4,2},{5,3},{6,4},{7,5},{8,14},{9,15},{10,... | collective-permute-start | bytes 73736 | tf_op jit(solution)/shard_map/ppermute | solution.py:133
  4.6 3.8 %collective-permute-done.1 = bf16[3,32,128]{2,1,0:T(8,128)(2,1)S(1)} collective-permute-done((bf16[3,32,128]{2,1,0:T(8,128)(2,1)}, bf16[3,32,128]{2,1,0:T(8,128)(2,1)S(1)}, u32[]{:S(2)}, u32[]{:S(2)}) %collective-permute-start.1) | collective-permute-done | bytes 24608 | tf_op jit(solution)/shard_map/ppermute | solution.py:133
  9.7 4.1 %collective-permute-start.5 = (bf16[4,3,32,128]{3,2,1,0:T(8,128)(2,1)S(1)}, bf16[4,3,32,128]{3,2,1,0:T(8,128)(2,1)S(1)}, u32[]{:S(2)}, u32[]{:S(2)}) collective-permute-start(bf16[4,3,32,128]{3,2,1,0:T(8,128)(2,1)S(1)} %get-tuple-element.57), channel_id=1, source_target_pairs={{0,24},{1,25},{2,26},{3,27},{4,28},{5,29},{6,30},{7,31},{8,0},{9,1... | collective-permute-start | bytes 294920 | tf_op jit(solution)/shard_map/ppermute | solution.py:130
  15.0 4.7 %slice.88 = bf16[32,2,2,128,128]{4,3,2,1,0:T(8,128)(2,1)} slice(bf16[32,2,3,128,128]{4,3,2,1,0:T(8,128)(2,1)} %bitcast.97), slice={[0:32], [0:2], [0:2], [0:128], [0:128]} | slice | bytes 8388608 | tf_op jit(solution)/shard_map/slice | solution.py:143
  20.7 4.9 %all-to-all-start = ((bf16[32,2,2,128,128]{4,3,2,1,0:T(8,128)(2,1)}), bf16[32,2,2,128,128]{4,3,2,1,0:T(8,128)(2,1)}, u32[]{:S(2)}, u32[]{:S(2)}) async-start(bf16[32,2,2,128,128]{4,3,2,1,0:T(8,128)(2,1)} %slice.88), calls=%async_computation | async-start | bytes 8388608 | tf_op jit(solution)/shard_map/all_to_all | solution.py:151
  25.6 3.2 %slice.89 = bf16[32,2,1,128,128]{4,3,2,1,0:T(8,128)(2,1)} slice(bf16[32,2,3,128,128]{4,3,2,1,0:T(8,128)(2,1)} %bitcast.98), slice={[0:32], [0:2], [2:3], [0:128], [0:128]} | slice | bytes 4194304 | tf_op jit(solution)/shard_map/slice | solution.py:143
  28.8 3.0 %collective-permute-start.8 = (bf16[4,4,3,32,128]{4,3,2,1,0:T(8,128)(2,1)S(1)}, bf16[4,4,3,32,128]{4,3,2,1,0:T(8,128)(2,1)S(1)}, u32[]{:S(2)}, u32[]{:S(2)}) collective-permute-start(bf16[4,4,3,32,128]{4,3,2,1,0:T(8,128)(2,1)S(1)} %pad_maximum_fusion.1), channel_id=1, source_target_pairs={{0,96},{32,0},{64,32},{96,64},{1,97},{33,1},{65,33},{97,65},{2,98}... | collective-permute-start | bytes 1179656 | tf_op jit(solution)/shard_map/ppermute | solution.py:127
  33.4 11.9 %copy.32.tiles_ref = bf16[32,128,1024]{2,1,0:T(8,128)(2,1)} copy(bf16[32,128,1024]{1,2,0:T(8,128)(2,1)} %bitcast.96) | data formatting | bytes 16777216 | tf_op jit(solution)/shard_map/reshape | solution.py:153
  45.4 3.5 %collective-permute-done.8 = bf16[4,4,3,32,128]{4,3,2,1,0:T(8,128)(2,1)S(1)} collective-permute-done((bf16[4,4,3,32,128]{4,3,2,1,0:T(8,128)(2,1)S(1)}, bf16[4,4,3,32,128]{4,3,2,1,0:T(8,128)(2,1)S(1)}, u32[]{:S(2)}, u32[]{:S(2)}) %collective-permute-start.8) | collective-permute-done | bytes 393248 | tf_op jit(solution)/shard_map/ppermute | solution.py:127
  48.9 3.7 %collective-permute-done.6 = bf16[4,4,3,32,128]{4,3,2,1,0:T(8,128)(2,1)S(1)} collective-permute-done((bf16[4,4,3,32,128]{4,3,2,1,0:T(8,128)(2,1)S(1)}, bf16[4,4,3,32,128]{4,3,2,1,0:T(8,128)(2,1)S(1)}, u32[]{:S(2)}, u32[]{:S(2)}) %collective-permute-start.6) | collective-permute-done | bytes 393248 | tf_op jit(solution)/shard_map/ppermute | solution.py:127
  53.3 26.2 %all-to-all-done.ens_ref = bf16[32,2,2,128,128]{4,3,2,1,0:T(8,128)(2,1)} async-done(((bf16[32,2,2,128,128]{4,3,2,1,0:T(8,128)(2,1)}), bf16[32,2,2,128,128]{4,3,2,1,0:T(8,128)(2,1)}, u32[]{:S(2)}, u32[]{:S(2)}) %all-to-all-start) | async-done | bytes 4194336 | tf_op jit(solution)/shard_map/all_to_all | solution.py:151
  79.6 4.8 %all-to-all-start.1 = ((bf16[32,2,1,128,128]{4,3,2,1,0:T(8,128)(2,1)}), bf16[32,2,1,128,128]{4,3,2,1,0:T(8,128)(2,1)}, u32[]{:S(2)}, u32[]{:S(2)}) async-start(bf16[32,2,1,128,128]{4,3,2,1,0:T(8,128)(2,1)} %slice.89), calls=%async_computation.1 | async-start | bytes 4194304 | tf_op jit(solution)/shard_map/all_to_all | solution.py:158
  84.7 16.3 %members_0.1 = (bf16[4,4,4,32,128]{4,3,2,1,0:T(8,128)(2,1)S(1)}, bf16[4,4,4,32,128]{4,3,2,1,0:T(8,128)(2,1)S(1)}) custom-call(s32[4]{0:T(128)S(1)} %pad_add_fusion.where_ref, s32[32,8]{1,0:T(8,128)S(1)} %copy.20.cols_ref, bf16[32,2,2,128,128]{4,3,2,1,0:T(8,128)(2,1)} %all-to-all-done.ens_ref, bf16[4,4,4,3,32,128]{5,4,3,2,1,0:T(8,128)(2,1)S(1)} %pad_maximum_fusion.mine_ref, ...), custom_call_target="tpu_custom_call" | custom-call | tf_op jit(solution)/shard_map/members_0/pallas_call | solution.py:181
  101.1 16.2 %members_1.1 = (bf16[4,4,4,32,128]{4,3,2,1,0:T(8,128)(2,1)S(1)}, bf16[4,4,4,32,128]{4,3,2,1,0:T(8,128)(2,1)S(1)}) custom-call(s32[4]{0:T(128)S(1)} %pad_add_fusion.where_ref, s32[32,8]{1,0:T(8,128)S(1)} %copy.20.cols_ref, bf16[32,2,2,128,128]{4,3,2,1,0:T(8,128)(2,1)} %all-to-all-done.ens_ref, bf16[4,4,4,3,32,128]{5,4,3,2,1,0:T(8,128)(2,1)S(1)} %pad_maximum_fusion.mine_ref, ...), custom_call_target="tpu_custom_call" | custom-call | tf_op jit(solution)/shard_map/members_1/pallas_call | solution.py:181
  118.1 3.1 %collective-permute-start.13 = (bf16[4,4,32,128]{3,2,1,0:T(8,128)(2,1)S(1)}, bf16[4,4,32,128]{3,2,1,0:T(8,128)(2,1)S(1)}, u32[]{:S(2)}, u32[]{:S(2)}) collective-permute-start(bf16[4,4,32,128]{3,2,1,0:T(8,128)(2,1)S(1)} %get-tuple-element.48), channel_id=1, source_target_pairs={{0,96},{32,0},{64,32},{96,64},{1,97},{33,1},{65,33},{97,65},{2,98}... | collective-permute-start | bytes 393224 | tf_op jit(solution)/shard_map/ppermute | solution.py:127
  123.0 2.3 %collective-permute-start.17 = (bf16[4,4,32,128]{3,2,1,0:T(8,128)(2,1)S(1)}, bf16[4,4,32,128]{3,2,1,0:T(8,128)(2,1)S(1)}, u32[]{:S(2)}, u32[]{:S(2)}) collective-permute-start(bf16[4,4,32,128]{3,2,1,0:T(8,128)(2,1)S(1)} %get-tuple-element.45), channel_id=1, source_target_pairs={{0,96},{32,0},{64,32},{96,64},{1,97},{33,1},{65,33},{97,65},{2,98}... | collective-permute-start | bytes 393224 | tf_op jit(solution)/shard_map/ppermute | solution.py:127
  129.0 3.5 %collective-permute-done.11 = bf16[4,4,32,128]{3,2,1,0:T(8,128)(2,1)S(1)} collective-permute-done((bf16[4,4,32,128]{3,2,1,0:T(8,128)(2,1)S(1)}, bf16[4,4,32,128]{3,2,1,0:T(8,128)(2,1)S(1)}, u32[]{:S(2)}, u32[]{:S(2)}) %collective-permute-start.11) | collective-permute-done | bytes 131104 | tf_op jit(solution)/shard_map/ppermute | solution.py:127
  137.0 15.6 %members_2.1 = (bf16[4,4,4,32,128]{4,3,2,1,0:T(8,128)(2,1)S(1)}, bf16[4,4,4,32,128]{4,3,2,1,0:T(8,128)(2,1)S(1)}) custom-call(s32[4]{0:T(128)S(1)} %pad_add_fusion.where_ref, s32[32,8]{1,0:T(8,128)S(1)} %copy.20.cols_ref, bf16[32,2,1,128,128]{4,3,2,1,0:T(8,128)(2,1)} %all-to-all-done.1.ens_ref, bf16[4,4,4,3,32,128]{5,4,3,2,1,0:T(8,128)(2,1)S(1)} %pad_maximum_fusion.mine_ref, ...), custom_call_target="tpu_custom_call" | custom-call | tf_op jit(solution)/shard_map/members_2/pallas_call | solution.py:181
  157.2 4.3 %collective-permute-done.21 = bf16[4,4,32,128]{3,2,1,0:T(8,128)(2,1)S(1)} collective-permute-done((bf16[4,4,32,128]{3,2,1,0:T(8,128)(2,1)S(1)}, bf16[4,4,32,128]{3,2,1,0:T(8,128)(2,1)S(1)}, u32[]{:S(2)}, u32[]{:S(2)}) %collective-permute-start.21) | collective-permute-done | bytes 131104 | tf_op jit(solution)/shard_map/ppermute | solution.py:127
  165.4 3.1 %collective-permute-start.24 = (bf16[4,3,32,128]{3,2,0,1:T(8,128)(2,1)S(1)}, bf16[4,3,32,128]{3,2,0,1:T(8,128)(2,1)S(1)}, u32[]{:S(2)}, u32[]{:S(2)}) collective-permute-start(bf16[4,3,32,128]{3,2,0,1:T(8,128)(2,1)S(1)} %get-tuple-element.51), channel_id=1, source_target_pairs={{0,24},{1,25},{2,26},{3,27},{4,28},{5,29},{6,30},{7,31},{8,0},{9,1... | collective-permute-start | bytes 294920 | tf_op jit(solution)/shard_map/ppermute | solution.py:130
  170.2 2.7 %collective-permute-done.24 = bf16[4,3,32,128]{3,2,0,1:T(8,128)(2,1)S(1)} collective-permute-done((bf16[4,3,32,128]{3,2,0,1:T(8,128)(2,1)S(1)}, bf16[4,3,32,128]{3,2,0,1:T(8,128)(2,1)S(1)}, u32[]{:S(2)}, u32[]{:S(2)}) %collective-permute-start.24) | collective-permute-done | bytes 98336 | tf_op jit(solution)/shard_map/ppermute | solution.py:130
  172.9 2.6 %collective-permute-done.23 = bf16[4,3,32,128]{3,2,0,1:T(8,128)(2,1)S(1)} collective-permute-done((bf16[4,3,32,128]{3,2,0,1:T(8,128)(2,1)S(1)}, bf16[4,3,32,128]{3,2,0,1:T(8,128)(2,1)S(1)}, u32[]{:S(2)}, u32[]{:S(2)}) %collective-permute-start.23) | collective-permute-done | bytes 98336 | tf_op jit(solution)/shard_map/ppermute | solution.py:130
  176.6 2.8 %collective-permute-start.27 = (bf16[3,32,128]{2,1,0:T(8,128)(2,1)S(1)}, bf16[3,32,128]{2,1,0:T(8,128)(2,1)S(1)}, u32[]{:S(2)}, u32[]{:S(2)}) collective-permute-start(bf16[3,32,128]{2,1,0:T(8,128)(2,1)S(1)} %get-tuple-element.54), channel_id=1, source_target_pairs={{0,6},{1,7},{2,0},{3,1},{4,2},{5,3},{6,4},{7,5},{8,14},{9,15},{10,... | collective-permute-start | bytes 73736 | tf_op jit(solution)/shard_map/ppermute | solution.py:133
  181.1 3.6 %collective-permute-done.26 = bf16[3,32,128]{2,1,0:T(8,128)(2,1)S(1)} collective-permute-done((bf16[3,32,128]{2,1,0:T(8,128)(2,1)S(1)}, bf16[3,32,128]{2,1,0:T(8,128)(2,1)S(1)}, u32[]{:S(2)}, u32[]{:S(2)}) %collective-permute-start.26) | collective-permute-done | bytes 24608 | tf_op jit(solution)/shard_map/ppermute | solution.py:133
  (74 shorter events, 32.8 us)
Async XLA Ops:
  2.9 5.5 %collective-permute-start.1 = (bf16[3,32,128]{2,1,0:T(8,128)(2,1)}, bf16[3,32,128]{2,1,0:T(8,128)(2,1)S(1)}, u32[]{:S(2)}, u32[]{:S(2)}) collective-permute-start(bf16[3,32,128]{2,1,0:T(8,128)(2,1)} %param.7), channel_id=1, source_target_pairs={{0,4},{1,5},{2,6},{3,7},{4,0},{5,1},{6,2},{7,3},{8,12},{9,13},{10,... | collective-permute-start | bytes 73736 | tf_op jit(solution)/shard_map/ppermute | solution.py:133
  9.7 10.1 %collective-permute-start.5 = (bf16[4,3,32,128]{3,2,1,0:T(8,128)(2,1)S(1)}, bf16[4,3,32,128]{3,2,1,0:T(8,128)(2,1)S(1)}, u32[]{:S(2)}, u32[]{:S(2)}) collective-permute-start(bf16[4,3,32,128]{3,2,1,0:T(8,128)(2,1)S(1)} %get-tuple-element.57), channel_id=1, source_target_pairs={{0,24},{1,25},{2,26},{3,27},{4,28},{5,29},{6,30},{7,31},{8,0},{9,1... | collective-permute-start | bytes 294920 | tf_op jit(solution)/shard_map/ppermute | solution.py:130
  13.8 6.2 %collective-permute-start.4 = (bf16[4,3,32,128]{3,2,1,0:T(8,128)(2,1)S(1)}, bf16[4,3,32,128]{3,2,1,0:T(8,128)(2,1)S(1)}, u32[]{:S(2)}, u32[]{:S(2)}) collective-permute-start(bf16[4,3,32,128]{3,2,1,0:T(8,128)(2,1)S(1)} %get-tuple-element.57), channel_id=1, source_target_pairs={{0,16},{1,17},{2,18},{3,19},{4,20},{5,21},{6,22},{7,23},{8,24},{9,... | collective-permute-start | bytes 294920 | tf_op jit(solution)/shard_map/ppermute | solution.py:130
  13.8 6.9 %collective-permute-start.3 = (bf16[4,3,32,128]{3,2,1,0:T(8,128)(2,1)S(1)}, bf16[4,3,32,128]{3,2,1,0:T(8,128)(2,1)S(1)}, u32[]{:S(2)}, u32[]{:S(2)}) collective-permute-start(bf16[4,3,32,128]{3,2,1,0:T(8,128)(2,1)S(1)} %get-tuple-element.57), channel_id=1, source_target_pairs={{0,8},{1,9},{2,10},{3,11},{4,12},{5,13},{6,14},{7,15},{8,16},{9,17... | collective-permute-start | bytes 294920 | tf_op jit(solution)/shard_map/ppermute | solution.py:130
  20.7 58.8 %all-to-all-start = ((bf16[32,2,2,128,128]{4,3,2,1,0:T(8,128)(2,1)}), bf16[32,2,2,128,128]{4,3,2,1,0:T(8,128)(2,1)}, u32[]{:S(2)}, u32[]{:S(2)}) async-start(bf16[32,2,2,128,128]{4,3,2,1,0:T(8,128)(2,1)} %slice.88), calls=%async_computation | async-start | bytes 8388608 | tf_op jit(solution)/shard_map/all_to_all | solution.py:151
  28.8 20.1 %collective-permute-start.8 = (bf16[4,4,3,32,128]{4,3,2,1,0:T(8,128)(2,1)S(1)}, bf16[4,4,3,32,128]{4,3,2,1,0:T(8,128)(2,1)S(1)}, u32[]{:S(2)}, u32[]{:S(2)}) collective-permute-start(bf16[4,4,3,32,128]{4,3,2,1,0:T(8,128)(2,1)S(1)} %pad_maximum_fusion.1), channel_id=1, source_target_pairs={{0,96},{32,0},{64,32},{96,64},{1,97},{33,1},{65,33},{97,65},{2,98}... | collective-permute-start | bytes 1179656 | tf_op jit(solution)/shard_map/ppermute | solution.py:127
  31.8 17.1 %collective-permute-start.7 = (bf16[4,4,3,32,128]{4,3,2,1,0:T(8,128)(2,1)S(1)}, bf16[4,4,3,32,128]{4,3,2,1,0:T(8,128)(2,1)S(1)}, u32[]{:S(2)}, u32[]{:S(2)}) collective-permute-start(bf16[4,4,3,32,128]{4,3,2,1,0:T(8,128)(2,1)S(1)} %pad_maximum_fusion.1), channel_id=1, source_target_pairs={{0,64},{32,96},{64,0},{96,32},{1,65},{33,97},{65,1},{97,33},{2,66}... | collective-permute-start | bytes 1179656 | tf_op jit(solution)/shard_map/ppermute | solution.py:127
  32.5 20.1 %collective-permute-start.6 = (bf16[4,4,3,32,128]{4,3,2,1,0:T(8,128)(2,1)S(1)}, bf16[4,4,3,32,128]{4,3,2,1,0:T(8,128)(2,1)S(1)}, u32[]{:S(2)}, u32[]{:S(2)}) collective-permute-start(bf16[4,4,3,32,128]{4,3,2,1,0:T(8,128)(2,1)S(1)} %pad_maximum_fusion.1), channel_id=1, source_target_pairs={{0,32},{32,64},{64,96},{96,0},{1,33},{33,65},{65,97},{97,1},{2,34}... | collective-permute-start | bytes 1179656 | tf_op jit(solution)/shard_map/ppermute | solution.py:127
  52.8 31.9 %collective-permute-start.9 = (bf16[4,4,4,3,32,128]{5,4,3,2,1,0:T(8,128)(2,1)S(1)}, bf16[4,4,4,3,32,128]{5,4,3,2,1,0:T(8,128)(2,1)S(1)}, u32[]{:S(2)}, u32[]{:S(2)}) collective-permute-start(bf16[4,4,4,3,32,128]{5,4,3,2,1,0:T(8,128)(2,1)S(1)} %pad_maximum_fusion.mine_ref), channel_id=1, source_target_pairs={{0,1},{1,0},{2,3},{3,2},{4,5},{5,4},{6,7},{7,6},{8,9},{9,8},{10,11... | collective-permute-start | bytes 4718600 | tf_op jit(solution)/shard_map/ppermute | solution.py:136
  79.6 57.5 %all-to-all-start.1 = ((bf16[32,2,1,128,128]{4,3,2,1,0:T(8,128)(2,1)}), bf16[32,2,1,128,128]{4,3,2,1,0:T(8,128)(2,1)}, u32[]{:S(2)}, u32[]{:S(2)}) async-start(bf16[32,2,1,128,128]{4,3,2,1,0:T(8,128)(2,1)} %slice.89), calls=%async_computation.1 | async-start | bytes 4194304 | tf_op jit(solution)/shard_map/all_to_all | solution.py:158
  100.9 16.9 %collective-permute-start.10 = (bf16[4,4,4,32,128]{4,3,2,1,0:T(8,128)(2,1)S(1)}, bf16[4,4,4,32,128]{4,3,2,1,0:T(8,128)(2,1)S(1)}, u32[]{:S(2)}, u32[]{:S(2)}) collective-permute-start(bf16[4,4,4,32,128]{4,3,2,1,0:T(8,128)(2,1)S(1)} %get-tuple-element.33), channel_id=1, source_target_pairs={{0,1},{1,0},{2,3},{3,2},{4,5},{5,4},{6,7},{7,6},{8,9},{9,8},{10,11... | collective-permute-start | bytes 1572872 | tf_op jit(solution)/shard_map/ppermute | solution.py:136
  117.4 5.4 %collective-permute-start.14 = (bf16[4,4,4,32,128]{4,3,2,1,0:T(8,128)(2,1)S(1)}, bf16[4,4,4,32,128]{4,3,2,1,0:T(8,128)(2,1)S(1)}, u32[]{:S(2)}, u32[]{:S(2)}) collective-permute-start(bf16[4,4,4,32,128]{4,3,2,1,0:T(8,128)(2,1)S(1)} %get-tuple-element.35), channel_id=1, source_target_pairs={{0,1},{1,0},{2,3},{3,2},{4,5},{5,4},{6,7},{7,6},{8,9},{9,8},{10,11... | collective-permute-start | bytes 1572872 | tf_op jit(solution)/shard_map/ppermute | solution.py:136
  118.1 9.8 %collective-permute-start.13 = (bf16[4,4,32,128]{3,2,1,0:T(8,128)(2,1)S(1)}, bf16[4,4,32,128]{3,2,1,0:T(8,128)(2,1)S(1)}, u32[]{:S(2)}, u32[]{:S(2)}) collective-permute-start(bf16[4,4,32,128]{3,2,1,0:T(8,128)(2,1)S(1)} %get-tuple-element.48), channel_id=1, source_target_pairs={{0,96},{32,0},{64,32},{96,64},{1,97},{33,1},{65,33},{97,65},{2,98}... | collective-permute-start | bytes 393224 | tf_op jit(solution)/shard_map/ppermute | solution.py:127
  121.2 7.9 %collective-permute-start.12 = (bf16[4,4,32,128]{3,2,1,0:T(8,128)(2,1)S(1)}, bf16[4,4,32,128]{3,2,1,0:T(8,128)(2,1)S(1)}, u32[]{:S(2)}, u32[]{:S(2)}) collective-permute-start(bf16[4,4,32,128]{3,2,1,0:T(8,128)(2,1)S(1)} %get-tuple-element.49), channel_id=1, source_target_pairs={{0,64},{32,96},{64,0},{96,32},{1,65},{33,97},{65,1},{97,33},{2,66}... | collective-permute-start | bytes 393224 | tf_op jit(solution)/shard_map/ppermute | solution.py:127
  121.8 10.7 %collective-permute-start.11 = (bf16[4,4,32,128]{3,2,1,0:T(8,128)(2,1)S(1)}, bf16[4,4,32,128]{3,2,1,0:T(8,128)(2,1)S(1)}, u32[]{:S(2)}, u32[]{:S(2)}) collective-permute-start(bf16[4,4,32,128]{3,2,1,0:T(8,128)(2,1)S(1)} %get-tuple-element.47), channel_id=1, source_target_pairs={{0,32},{32,64},{64,96},{96,0},{1,33},{33,65},{65,97},{97,1},{2,34}... | collective-permute-start | bytes 393224 | tf_op jit(solution)/shard_map/ppermute | solution.py:127
  123.0 9.6 %collective-permute-start.17 = (bf16[4,4,32,128]{3,2,1,0:T(8,128)(2,1)S(1)}, bf16[4,4,32,128]{3,2,1,0:T(8,128)(2,1)S(1)}, u32[]{:S(2)}, u32[]{:S(2)}) collective-permute-start(bf16[4,4,32,128]{3,2,1,0:T(8,128)(2,1)S(1)} %get-tuple-element.45), channel_id=1, source_target_pairs={{0,96},{32,0},{64,32},{96,64},{1,97},{33,1},{65,33},{97,65},{2,98}... | collective-permute-start | bytes 393224 | tf_op jit(solution)/shard_map/ppermute | solution.py:127
  125.3 9.4 %collective-permute-start.16 = (bf16[4,4,32,128]{3,2,1,0:T(8,128)(2,1)S(1)}, bf16[4,4,32,128]{3,2,1,0:T(8,128)(2,1)S(1)}, u32[]{:S(2)}, u32[]{:S(2)}) collective-permute-start(bf16[4,4,32,128]{3,2,1,0:T(8,128)(2,1)S(1)} %get-tuple-element.46), channel_id=1, source_target_pairs={{0,64},{32,96},{64,0},{96,32},{1,65},{33,97},{65,1},{97,33},{2,66}... | collective-permute-start | bytes 393224 | tf_op jit(solution)/shard_map/ppermute | solution.py:127
  127.8 8.5 %collective-permute-start.15 = (bf16[4,4,32,128]{3,2,1,0:T(8,128)(2,1)S(1)}, bf16[4,4,32,128]{3,2,1,0:T(8,128)(2,1)S(1)}, u32[]{:S(2)}, u32[]{:S(2)}) collective-permute-start(bf16[4,4,32,128]{3,2,1,0:T(8,128)(2,1)S(1)} %get-tuple-element.44), channel_id=1, source_target_pairs={{0,32},{32,64},{64,96},{96,0},{1,33},{33,65},{65,97},{97,1},{2,34}... | collective-permute-start | bytes 393224 | tf_op jit(solution)/shard_map/ppermute | solution.py:127
  155.1 6.4 %collective-permute-start.21 = (bf16[4,4,32,128]{3,2,1,0:T(8,128)(2,1)S(1)}, bf16[4,4,32,128]{3,2,1,0:T(8,128)(2,1)S(1)}, u32[]{:S(2)}, u32[]{:S(2)}) collective-permute-start(bf16[4,4,32,128]{3,2,1,0:T(8,128)(2,1)S(1)} %get-tuple-element.42), channel_id=1, source_target_pairs={{0,96},{32,0},{64,32},{96,64},{1,97},{33,1},{65,33},{97,65},{2,98}... | collective-permute-start | bytes 393224 | tf_op jit(solution)/shard_map/ppermute | solution.py:127
  155.7 7.8 %collective-permute-start.20 = (bf16[4,4,32,128]{3,2,1,0:T(8,128)(2,1)S(1)}, bf16[4,4,32,128]{3,2,1,0:T(8,128)(2,1)S(1)}, u32[]{:S(2)}, u32[]{:S(2)}) collective-permute-start(bf16[4,4,32,128]{3,2,1,0:T(8,128)(2,1)S(1)} %get-tuple-element.43), channel_id=1, source_target_pairs={{0,64},{32,96},{64,0},{96,32},{1,65},{33,97},{65,1},{97,33},{2,66}... | collective-permute-start | bytes 393224 | tf_op jit(solution)/shard_map/ppermute | solution.py:127
  156.3 9.0 %collective-permute-start.19 = (bf16[4,4,32,128]{3,2,1,0:T(8,128)(2,1)S(1)}, bf16[4,4,32,128]{3,2,1,0:T(8,128)(2,1)S(1)}, u32[]{:S(2)}, u32[]{:S(2)}) collective-permute-start(bf16[4,4,32,128]{3,2,1,0:T(8,128)(2,1)S(1)} %get-tuple-element.41), channel_id=1, source_target_pairs={{0,32},{32,64},{64,96},{96,0},{1,33},{33,65},{65,97},{97,1},{2,34}... | collective-permute-start | bytes 393224 | tf_op jit(solution)/shard_map/ppermute | solution.py:127
  165.4 7.5 %collective-permute-start.24 = (bf16[4,3,32,128]{3,2,0,1:T(8,128)(2,1)S(1)}, bf16[4,3,32,128]{3,2,0,1:T(8,128)(2,1)S(1)}, u32[]{:S(2)}, u32[]{:S(2)}) collective-permute-start(bf16[4,3,32,128]{3,2,0,1:T(8,128)(2,1)S(1)} %get-tuple-element.51), channel_id=1, source_target_pairs={{0,24},{1,25},{2,26},{3,27},{4,28},{5,29},{6,30},{7,31},{8,0},{9,1... | collective-permute-start | bytes 294920 | tf_op jit(solution)/shard_map/ppermute | solution.py:130
  168.5 7.0 %collective-permute-start.23 = (bf16[4,3,32,128]{3,2,0,1:T(8,128)(2,1)S(1)}, bf16[4,3,32,128]{3,2,0,1:T(8,128)(2,1)S(1)}, u32[]{:S(2)}, u32[]{:S(2)}) collective-permute-start(bf16[4,3,32,128]{3,2,0,1:T(8,128)(2,1)S(1)} %get-tuple-element.52), channel_id=1, source_target_pairs={{0,16},{1,17},{2,18},{3,19},{4,20},{5,21},{6,22},{7,23},{8,24},{9,... | collective-permute-start | bytes 294920 | tf_op jit(solution)/shard_map/ppermute | solution.py:130
  169.3 7.3 %collective-permute-start.22 = (bf16[4,3,32,128]{3,2,0,1:T(8,128)(2,1)S(1)}, bf16[4,3,32,128]{3,2,0,1:T(8,128)(2,1)S(1)}, u32[]{:S(2)}, u32[]{:S(2)}) collective-permute-start(bf16[4,3,32,128]{3,2,0,1:T(8,128)(2,1)S(1)} %get-tuple-element.50), channel_id=1, source_target_pairs={{0,8},{1,9},{2,10},{3,11},{4,12},{5,13},{6,14},{7,15},{8,16},{9,17... | collective-permute-start | bytes 294920 | tf_op jit(solution)/shard_map/ppermute | solution.py:130
  (10 other events, 102.5 us)

commit v3 on v2

--- a/solution.py
+++ b/solution.py
@@ -7,15 +7,17 @@
 from jax.experimental.pallas import tpu as pltpu
 from jax.sharding import PartitionSpec as P
 
+
 BF = jnp.bfloat16
 F32 = jnp.float32
 CORES = 2
 FLOOR = 2
+UNROLL = 4
 
 
 def member_kernel(
     where_ref, cols_ref, ens_ref, mine_ref, other_ref, vt_ref, vn_ref, mask_ref, tiles_ref,
-    near_ref, far_ref, tile_buf, lifted, sems, *, var, slot_of_var,
+    near_ref, far_ref, tile_buf, lifted, spread_buf, sems, *, var, slot_of_var,
 ):
     members = ens_ref.shape[1]
     n_blocks = ens_ref.shape[0]
@@ -70,7 +72,7 @@
     for piece in range(n_copies):
         tile_copy(piece).wait()
 
-    def spread_block(target_ref, block, off_z, off_x):
+    def spread_block(block):
         parts = []
         for slot in range(slots):
             picked = lifted[cols_ref[block, slot]]
@@ -80,9 +82,17 @@
         spread = jnp.dot(
             tile_buf[block], jnp.concatenate(parts, axis=0), preferred_element_type=F32
         ).astype(BF)
-        beside = jnp.concatenate(
-            [spread[:, m * levels:(m + 1) * levels] for m in range(members)], axis=0
-        )
+        for m in range(members):
+            spread_buf[block, m * width:(m + 1) * width, :] = spread[:, m * levels:(m + 1) * levels]
+
+    def spread_step(step, carry):
+        spread_block(step)
+        return carry
+
+    lax.fori_loop(0, n_blocks, spread_step, 0, unroll=UNROLL)
+
+    def lower_block(target_ref, block, off_z, off_x):
+        beside = spread_buf[block]
         lowered = lax.dot_general(
             vn_ref[var], beside, (((1,), (1,)), ((), ())), preferred_element_type=F32
         )
@@ -95,13 +105,13 @@
             off_y = lax.rem(quarter - my_y + y_n, y_n)
             target_ref[off_y, off_z, off_x] = total[quarter * part_l:(quarter + 1) * part_l, :]
 
-    def spread_step(step, carry):
+    def lower_step(step, carry):
         off_z, off_x, base = seat_of(step)
-        spread_block(near_ref, base + my_c, off_z, off_x)
-        spread_block(far_ref, base + 1 - my_c, off_z, off_x)
+        lower_block(near_ref, base + my_c, off_z, off_x)
+        lower_block(far_ref, base + 1 - my_c, off_z, off_x)
         return carry
 
-    lax.fori_loop(0, n_blocks // CORES, spread_step, 0, unroll=2)
+    lax.fori_loop(0, n_blocks // CORES, lower_step, 0, unroll=2)
 
 
 def on_device(
@@ -146,8 +156,8 @@
     }
 
     mine = collect(increment, shift_x, x_n)
+    pieces[0], mine = lax.optimization_barrier((pieces[0], mine))
     mine = collect(mine, shift_z, z_n)
-    pieces[0], mine = lax.optimization_barrier((pieces[0], mine))
     arrived = [lax.all_to_all(pieces[0], "col", 0, 0)]
     mine, pieces[1], tiles = lax.optimization_barrier((mine, pieces[1], tiles))
     turned_tiles = jnp.transpose(tiles, (0, 3, 1, 2)).reshape(columns, width, slots * width)
@@ -173,11 +183,13 @@
             total = total + p.astype(F32)
         return total
 
-    held = []
+    chips = []
     for var in range(n_var):
         index, place = where_var[var]
         if index and place == 0:
-            arrived[index], *held = lax.optimization_barrier((arrived[index], *held))
+            early = jnp.stack(chips, axis=3)
+            early = add([early[0]] + [shift_y(early[s], s) for s in range(1, y_n)]).astype(BF)
+            chips = []
         near, far = pl.pallas_call(
             functools.partial(member_kernel, var=var, slot_of_var=place),
             out_shape=(out, out),
@@ -187,14 +199,15 @@
             scratch_shapes=[
                 pltpu.VMEM(turned_tiles.shape, BF),
                 pltpu.VMEM((columns, width, members * levels), BF),
+                pltpu.VMEM((columns, members * width, levels), BF),
                 pltpu.SemaphoreType.DMA((4,)),
             ],
             compiler_params=pltpu.CompilerParams(vmem_limit_bytes=40 << 20),
-            name=f"members_{var}",
         )(where, tile_col, arrived[index], mine, other, vert_t, vert_root, mask, turned_tiles)
-        chip = add([near, swap(far)]).astype(BF)
-        held.append(add([chip[0]] + [shift_y(chip[s], s) for s in range(1, y_n)]).astype(BF))
-    held = jnp.stack(held, axis=2)
+        chips.append(add([near, swap(far)]).astype(BF))
+    late = jnp.stack(chips, axis=3)
+    late = add([late[0]] + [shift_y(late[s], s) for s in range(1, y_n)]).astype(BF)
+    held = jnp.concatenate([early, late], axis=2)
     held = add([held[0]] + [shift_z(held[s], s) for s in range(1, z_n)]).astype(BF)
     held = add([held[0]] + [shift_x(held[s], s) for s in range(1, x_n)])
     return (held / (members_all - 1)).astype(BF)

time: 187 us -> 185 us (0.989)
  Pallas kernels: 48.1 us -> 34.9 us
  waiting for transfers between devices: 68.5 us -> 81 us
  starting transfers between devices: 45.4 us -> 42.6 us
    ppermute x6, waiting for transfers between devices: 7.28 us -> 50.6 us  [shift_z(): lax.ppermute(a, 'col', [(seat(*p), seat(p[0] + s, p[1], p[2])) for p in s...]
    all_to_all x1, waiting for transfers between devices: 26.2 us -> 0.01 us  [on_device(): arrived = [lax.all_to_all(pieces[0], 'col', 0, 0)]]
    pallas_call x3, Pallas kernels: 48.1 us -> 34.9 us  [on_device(): pl.pallas_call(functools.partial(member_kernel, var=var, slot_of_var=plac...]
    ppermute x12 -> x9, starting transfers between devices: 15.4 us -> 11.3 us  [shift_y(): return lax.ppermute(a, 'mem', [(i, (i + s) % y_n) for i in range(y_n)])]
    all_to_all x1, waiting for transfers between devices: 0.01 us -> 3.27 us  [on_device(): arrived.append(lax.all_to_all(pieces[1], 'col', 0, 0))]
    ppermute x6, waiting for transfers between devices: 8.53 us -> 5.33 us  [shift_x(): lax.ppermute(a, 'col', [(seat(*p), seat(p[0], p[1] + s, p[2])) for p in s...]
    ppermute x12 -> x9, waiting for transfers between devices: 24.6 us -> 21.8 us  [shift_y(): return lax.ppermute(a, 'mem', [(i, (i + s) % y_n) for i in range(y_n)])]
    all_to_all x1, starting transfers between devices: 4.77 us -> 7.17 us  [on_device(): arrived.append(lax.all_to_all(pieces[1], 'col', 0, 0))]
  transfers between devices with their start and end apart: 30 -> 27, of which waited for: 21 -> 14; matrix products, arithmetic and copies ran while one was open for 12% -> 13% of each run, Pallas kernels for 17% -> 19%
where the time goes in v3:
time: 185 us
  waiting for transfers between devices  81 us (44%)
  starting transfers between devices  42.6 us (23%)
  Pallas kernels  34.9 us (19%)
  local copies, waits for them, and re-layouts  21.8 us (12%)
  other arithmetic  4 us (2%)
    ppermute x6, waiting for transfers between devices, shift_z(): lax.ppermute(a, 'col', [(seat(*p), seat(p[0] + s, p[1], p[2])) for p in s...  50.6 us
    pallas_call x3, Pallas kernels, on_device(): pl.pallas_call(functools.partial(member_kernel, var=var, slot_of_var=plac...  34.9 us
    ppermute x9, waiting for transfers between devices, shift_y(): return lax.ppermute(a, 'mem', [(i, (i + s) % y_n) for i in range(y_n)])  21.8 us
    reshape x1, local copies, waits for them, and re-layouts, on_device(): jnp.transpose(tiles, (0, 3, 1, 2)).reshape(columns, width, slots * width)  11.9 us
    ppermute x9, starting transfers between devices, shift_y(): return lax.ppermute(a, 'mem', [(i, (i + s) % y_n) for i in range(y_n)])  11.3 us
    ppermute x6, starting transfers between devices, shift_x(): lax.ppermute(a, 'col', [(seat(*p), seat(p[0], p[1] + s, p[2])) for p in s...  8.46 us
    ppermute x6, starting transfers between devices, shift_z(): lax.ppermute(a, 'col', [(seat(*p), seat(p[0] + s, p[1], p[2])) for p in s...  8.02 us
    slice x2, local copies, waits for them, and re-layouts, on_device(): pieces = [by_member[:, :, group[0]:group[-1] + 1] for group in groups]  7.92 us
  transfers between devices with their start and end apart: 27, of which 14 were waited for; matrix products, arithmetic and copies ran while one was open for 13% of the time, Pallas kernels for 19%

profile of v3, /device:TPU:0, one launch (start us, length us, event | category | flops | bytes accessed | tf_op | source)
XLA Modules:
  0.0 184.6 jit_solution(10517647105326429137)
XLA Ops:
  5.2 4.7 %slice.76 = bf16[32,2,2,128,128]{4,3,2,1,0:T(8,128)(2,1)} slice(bf16[32,2,3,128,128]{4,3,2,1,0:T(8,128)(2,1)} %bitcast.91), slice={[0:32], [0:2], [0:2], [0:128], [0:128]} | slice | bytes 8388608 | tf_op jit(solution)/shard_map/slice | solution.py:153
  9.9 7.0 %all-to-all-start = ((bf16[32,2,2,128,128]{4,3,2,1,0:T(8,128)(2,1)}), bf16[32,2,2,128,128]{4,3,2,1,0:T(8,128)(2,1)}, u32[]{:S(2)}, u32[]{:S(2)}) async-start(bf16[32,2,2,128,128]{4,3,2,1,0:T(8,128)(2,1)} %slice.76), calls=%async_computation | async-start | bytes 8388608 | tf_op jit(solution)/shard_map/all_to_all | solution.py:161
  16.9 3.0 %collective-permute-start.5 = (bf16[4,3,32,128]{3,2,1,0:T(8,128)(2,1)S(1)}, bf16[4,3,32,128]{3,2,1,0:T(8,128)(2,1)S(1)}, u32[]{:S(2)}, u32[]{:S(2)}) collective-permute-start(bf16[4,3,32,128]{3,2,1,0:T(8,128)(2,1)S(1)} %pad_maximum_fusion.4), channel_id=1, source_target_pairs={{0,24},{1,25},{2,26},{3,27},{4,28},{5,29},{6,30},{7,31},{8,0},{9,1... | collective-permute-start | bytes 294920 | tf_op jit(solution)/shard_map/ppermute | solution.py:140
  21.7 3.2 %slice.77 = bf16[32,2,1,128,128]{4,3,2,1,0:T(8,128)(2,1)} slice(bf16[32,2,3,128,128]{4,3,2,1,0:T(8,128)(2,1)} %bitcast.92), slice={[0:32], [0:2], [2:3], [0:128], [0:128]} | slice | bytes 4194304 | tf_op jit(solution)/shard_map/slice | solution.py:153
  24.9 42.0 %collective-permute-done.5 = bf16[4,3,32,128]{3,2,1,0:T(8,128)(2,1)S(1)} collective-permute-done((bf16[4,3,32,128]{3,2,1,0:T(8,128)(2,1)S(1)}, bf16[4,3,32,128]{3,2,1,0:T(8,128)(2,1)S(1)}, u32[]{:S(2)}, u32[]{:S(2)}) %collective-permute-start.5) | collective-permute-done | bytes 98336 | tf_op jit(solution)/shard_map/ppermute | solution.py:140
  69.4 3.1 %collective-permute-start.8 = (bf16[4,4,3,32,128]{4,3,2,1,0:T(8,128)(2,1)S(1)}, bf16[4,4,3,32,128]{4,3,2,1,0:T(8,128)(2,1)S(1)}, u32[]{:S(2)}, u32[]{:S(2)}) collective-permute-start(bf16[4,4,3,32,128]{4,3,2,1,0:T(8,128)(2,1)S(1)} %pad_maximum_fusion.1), channel_id=1, source_target_pairs={{0,96},{32,0},{64,32},{96,64},{1,97},{33,1},{65,33},{97,65},{2,98}... | collective-permute-start | bytes 1179656 | tf_op jit(solution)/shard_map/ppermute | solution.py:137
  74.1 11.9 %copy.38.tiles_ref = bf16[32,128,1024]{2,1,0:T(8,128)(2,1)} copy(bf16[32,128,1024]{1,2,0:T(8,128)(2,1)} %bitcast.90) | data formatting | bytes 16777216 | tf_op jit(solution)/shard_map/reshape | solution.py:163
  86.0 2.5 %collective-permute-done.8 = bf16[4,4,3,32,128]{4,3,2,1,0:T(8,128)(2,1)S(1)} collective-permute-done((bf16[4,4,3,32,128]{4,3,2,1,0:T(8,128)(2,1)S(1)}, bf16[4,4,3,32,128]{4,3,2,1,0:T(8,128)(2,1)S(1)}, u32[]{:S(2)}, u32[]{:S(2)}) %collective-permute-start.8) | collective-permute-done | bytes 393248 | tf_op jit(solution)/shard_map/ppermute | solution.py:137
  88.5 3.7 %collective-permute-done.6 = bf16[4,4,3,32,128]{4,3,2,1,0:T(8,128)(2,1)S(1)} collective-permute-done((bf16[4,4,3,32,128]{4,3,2,1,0:T(8,128)(2,1)S(1)}, bf16[4,4,3,32,128]{4,3,2,1,0:T(8,128)(2,1)S(1)}, u32[]{:S(2)}, u32[]{:S(2)}) %collective-permute-start.6) | collective-permute-done | bytes 393248 | tf_op jit(solution)/shard_map/ppermute | solution.py:137
  92.6 7.2 %all-to-all-start.1 = ((bf16[32,2,1,128,128]{4,3,2,1,0:T(8,128)(2,1)}), bf16[32,2,1,128,128]{4,3,2,1,0:T(8,128)(2,1)}, u32[]{:S(2)}, u32[]{:S(2)}) async-start(bf16[32,2,1,128,128]{4,3,2,1,0:T(8,128)(2,1)} %slice.77), calls=%async_computation.1 | async-start | bytes 4194304 | tf_op jit(solution)/shard_map/all_to_all | solution.py:168
  100.2 12.1 %shard_map.65 = (bf16[4,4,4,32,128]{4,3,2,1,0:T(8,128)(2,1)S(1)}, bf16[4,4,4,32,128]{4,3,2,1,0:T(8,128)(2,1)}) custom-call(s32[4]{0:T(128)S(1)} %pad_add_fusion.where_ref, s32[32,8]{1,0:T(8,128)S(1)} %copy.23.cols_ref, bf16[32,2,2,128,128]{4,3,2,1,0:T(8,128)(2,1)} %all-to-all-done.ens_ref, bf16[4,4,4,3,32,128]{5,4,3,2,1,0:T(8,128)(2,1)S(1)} %pad_maximum_fusion.mine_ref, ...), custom_call_target="tpu_custom_call" | custom-call | tf_op jit(solution)/shard_map/pallas_call | solution.py:193
  113.3 12.1 %shard_map.64 = (bf16[4,4,4,32,128]{4,3,2,1,0:T(8,128)(2,1)S(1)}, bf16[4,4,4,32,128]{4,3,2,1,0:T(8,128)(2,1)}) custom-call(s32[4]{0:T(128)S(1)} %pad_add_fusion.where_ref, s32[32,8]{1,0:T(8,128)S(1)} %copy.23.cols_ref, bf16[32,2,2,128,128]{4,3,2,1,0:T(8,128)(2,1)} %all-to-all-done.ens_ref, bf16[4,4,4,3,32,128]{5,4,3,2,1,0:T(8,128)(2,1)S(1)} %pad_maximum_fusion.mine_ref, ...), custom_call_target="tpu_custom_call" | custom-call | tf_op jit(solution)/shard_map/pallas_call | solution.py:193
  126.5 3.3 %all-to-all-done.1.ens_ref = bf16[32,2,1,128,128]{4,3,2,1,0:T(8,128)(2,1)} async-done(((bf16[32,2,1,128,128]{4,3,2,1,0:T(8,128)(2,1)}), bf16[32,2,1,128,128]{4,3,2,1,0:T(8,128)(2,1)}, u32[]{:S(2)}, u32[]{:S(2)}) %all-to-all-start.1) | async-done | bytes 2097184 | tf_op jit(solution)/shard_map/all_to_all | solution.py:168
  129.8 10.7 %shard_map.66 = (bf16[4,4,4,32,128]{4,3,2,1,0:T(8,128)(2,1)S(1)}, bf16[4,4,4,32,128]{4,3,2,1,0:T(8,128)(2,1)S(1)}) custom-call(s32[4]{0:T(128)S(1)} %pad_add_fusion.where_ref, s32[32,8]{1,0:T(8,128)S(1)} %copy.23.cols_ref, bf16[32,2,1,128,128]{4,3,2,1,0:T(8,128)(2,1)} %all-to-all-done.1.ens_ref, ...), custom_call_target="tpu_custom_call" | custom-call | tf_op jit(solution)/shard_map/pallas_call | solution.py:193
  143.3 3.2 %collective-permute-start.14 = (bf16[4,4,2,32,128]{4,3,1,0,2:T(8,128)(2,1)S(1)}, bf16[4,4,2,32,128]{4,3,1,0,2:T(8,128)(2,1)S(1)}, u32[]{:S(2)}, u32[]{:S(2)}) collective-permute-start(bf16[4,4,2,32,128]{4,3,1,0,2:T(8,128)(2,1)S(1)} %get-tuple-element.36), channel_id=1, source_target_pairs={{0,96},{32,0},{64,32},{96,64},{1,97},{33,1},{65,33},{97,65},{2,98}... | collective-permute-start | bytes 786440 | tf_op jit(solution)/shard_map/ppermute | solution.py:137
  147.6 2.4 %collective-permute-start.18 = (bf16[4,4,1,32,128]{4,3,1,0,2:T(8,128)(2,1)S(1)}, bf16[4,4,1,32,128]{4,3,1,0,2:T(8,128)(2,1)S(1)}, u32[]{:S(2)}, u32[]{:S(2)}) collective-permute-start(bf16[4,4,1,32,128]{4,3,1,0,2:T(8,128)(2,1)S(1)} %get-tuple-element.39), channel_id=1, source_target_pairs={{0,96},{32,0},{64,32},{96,64},{1,97},{33,1},{65,33},{97,65},{2,98}... | collective-permute-start | bytes 393224 | tf_op jit(solution)/shard_map/ppermute | solution.py:137
  150.0 9.3 %collective-permute-done.12 = bf16[4,4,2,32,128]{4,3,1,0,2:T(8,128)(2,1)S(1)} collective-permute-done((bf16[4,4,2,32,128]{4,3,1,0,2:T(8,128)(2,1)S(1)}, bf16[4,4,2,32,128]{4,3,1,0,2:T(8,128)(2,1)S(1)}, u32[]{:S(2)}, u32[]{:S(2)}) %collective-permute-start.12) | collective-permute-done | bytes 262176 | tf_op jit(solution)/shard_map/ppermute | solution.py:137
  159.4 2.1 %collective-permute-done.16 = bf16[4,4,1,32,128]{4,3,1,0,2:T(8,128)(2,1)S(1)} collective-permute-done((bf16[4,4,1,32,128]{4,3,1,0,2:T(8,128)(2,1)S(1)}, bf16[4,4,1,32,128]{4,3,1,0,2:T(8,128)(2,1)S(1)}, u32[]{:S(2)}, u32[]{:S(2)}) %collective-permute-start.16) | collective-permute-done | bytes 131104 | tf_op jit(solution)/shard_map/ppermute | solution.py:137
  163.6 2.1 %collective-permute-done.17 = bf16[4,4,1,32,128]{4,3,1,0,2:T(8,128)(2,1)S(1)} collective-permute-done((bf16[4,4,1,32,128]{4,3,1,0,2:T(8,128)(2,1)S(1)}, bf16[4,4,1,32,128]{4,3,1,0,2:T(8,128)(2,1)S(1)}, u32[]{:S(2)}, u32[]{:S(2)}) %collective-permute-start.17) | collective-permute-done | bytes 131104 | tf_op jit(solution)/shard_map/ppermute | solution.py:137
  165.9 3.2 %collective-permute-start.21 = (bf16[4,3,32,128]{3,2,0,1:T(8,128)(2,1)S(1)}, bf16[4,3,32,128]{3,2,0,1:T(8,128)(2,1)S(1)}, u32[]{:S(2)}, u32[]{:S(2)}) collective-permute-start(bf16[4,3,32,128]{3,2,0,1:T(8,128)(2,1)S(1)} %get-tuple-element.42), channel_id=1, source_target_pairs={{0,24},{1,25},{2,26},{3,27},{4,28},{5,29},{6,30},{7,31},{8,0},{9,1... | collective-permute-start | bytes 294920 | tf_op jit(solution)/shard_map/ppermute | solution.py:140
  169.2 3.6 %collective-permute-done.19 = bf16[4,3,32,128]{3,2,0,1:T(8,128)(2,1)S(1)} collective-permute-done((bf16[4,3,32,128]{3,2,0,1:T(8,128)(2,1)S(1)}, bf16[4,3,32,128]{3,2,0,1:T(8,128)(2,1)S(1)}, u32[]{:S(2)}, u32[]{:S(2)}) %collective-permute-start.19) | collective-permute-done | bytes 98336 | tf_op jit(solution)/shard_map/ppermute | solution.py:140
  172.7 2.6 %collective-permute-done.20 = bf16[4,3,32,128]{3,2,0,1:T(8,128)(2,1)S(1)} collective-permute-done((bf16[4,3,32,128]{3,2,0,1:T(8,128)(2,1)S(1)}, bf16[4,3,32,128]{3,2,0,1:T(8,128)(2,1)S(1)}, u32[]{:S(2)}, u32[]{:S(2)}) %collective-permute-start.20) | collective-permute-done | bytes 98336 | tf_op jit(solution)/shard_map/ppermute | solution.py:140
  175.4 3.2 %collective-permute-start.24 = (bf16[3,32,128]{2,1,0:T(8,128)(2,1)S(1)}, bf16[3,32,128]{2,1,0:T(8,128)(2,1)S(1)}, u32[]{:S(2)}, u32[]{:S(2)}) collective-permute-start(bf16[3,32,128]{2,1,0:T(8,128)(2,1)S(1)} %get-tuple-element.45), channel_id=1, source_target_pairs={{0,6},{1,7},{2,0},{3,1},{4,2},{5,3},{6,4},{7,5},{8,14},{9,15},{10,... | collective-permute-start | bytes 73736 | tf_op jit(solution)/shard_map/ppermute | solution.py:143
  180.5 3.5 %collective-permute-done.23 = bf16[3,32,128]{2,1,0:T(8,128)(2,1)S(1)} collective-permute-done((bf16[3,32,128]{2,1,0:T(8,128)(2,1)S(1)}, bf16[3,32,128]{2,1,0:T(8,128)(2,1)S(1)}, u32[]{:S(2)}, u32[]{:S(2)}) %collective-permute-start.23) | collective-permute-done | bytes 24608 | tf_op jit(solution)/shard_map/ppermute | solution.py:143
  (73 shorter events, 22.5 us)
Async XLA Ops:
  0.0 9.9 %collective-permute-start = (bf16[3,32,128]{2,1,0:T(8,128)(2,1)}, bf16[3,32,128]{2,1,0:T(8,128)(2,1)S(1)}, u32[]{:S(2)}, u32[]{:S(2)}) collective-permute-start(bf16[3,32,128]{2,1,0:T(8,128)(2,1)} %param.7), channel_id=1, source_target_pairs={{0,2},{1,3},{2,4},{3,5},{4,6},{5,7},{6,0},{7,1},{8,10},{9,11},{10,... | collective-permute-start | bytes 73736 | tf_op jit(solution)/shard_map/ppermute | solution.py:143
  1.6 8.3 %collective-permute-start.2 = (bf16[3,32,128]{2,1,0:T(8,128)(2,1)}, bf16[3,32,128]{2,1,0:T(8,128)(2,1)S(1)}, u32[]{:S(2)}, u32[]{:S(2)}) collective-permute-start(bf16[3,32,128]{2,1,0:T(8,128)(2,1)} %param.7), channel_id=1, source_target_pairs={{0,6},{1,7},{2,0},{3,1},{4,2},{5,3},{6,4},{7,5},{8,14},{9,15},{10,... | collective-permute-start | bytes 73736 | tf_op jit(solution)/shard_map/ppermute | solution.py:143
  3.2 6.7 %collective-permute-start.1 = (bf16[3,32,128]{2,1,0:T(8,128)(2,1)}, bf16[3,32,128]{2,1,0:T(8,128)(2,1)S(1)}, u32[]{:S(2)}, u32[]{:S(2)}) collective-permute-start(bf16[3,32,128]{2,1,0:T(8,128)(2,1)} %param.7), channel_id=1, source_target_pairs={{0,4},{1,5},{2,6},{3,7},{4,0},{5,1},{6,2},{7,3},{8,12},{9,13},{10,... | collective-permute-start | bytes 73736 | tf_op jit(solution)/shard_map/ppermute | solution.py:143
  9.9 82.6 %all-to-all-start = ((bf16[32,2,2,128,128]{4,3,2,1,0:T(8,128)(2,1)}), bf16[32,2,2,128,128]{4,3,2,1,0:T(8,128)(2,1)}, u32[]{:S(2)}, u32[]{:S(2)}) async-start(bf16[32,2,2,128,128]{4,3,2,1,0:T(8,128)(2,1)} %slice.76), calls=%async_computation | async-start | bytes 8388608 | tf_op jit(solution)/shard_map/all_to_all | solution.py:161
  16.9 49.9 %collective-permute-start.5 = (bf16[4,3,32,128]{3,2,1,0:T(8,128)(2,1)S(1)}, bf16[4,3,32,128]{3,2,1,0:T(8,128)(2,1)S(1)}, u32[]{:S(2)}, u32[]{:S(2)}) collective-permute-start(bf16[4,3,32,128]{3,2,1,0:T(8,128)(2,1)S(1)} %pad_maximum_fusion.4), channel_id=1, source_target_pairs={{0,24},{1,25},{2,26},{3,27},{4,28},{5,29},{6,30},{7,31},{8,0},{9,1... | collective-permute-start | bytes 294920 | tf_op jit(solution)/shard_map/ppermute | solution.py:140
  20.0 47.4 %collective-permute-start.4 = (bf16[4,3,32,128]{3,2,1,0:T(8,128)(2,1)S(1)}, bf16[4,3,32,128]{3,2,1,0:T(8,128)(2,1)S(1)}, u32[]{:S(2)}, u32[]{:S(2)}) collective-permute-start(bf16[4,3,32,128]{3,2,1,0:T(8,128)(2,1)S(1)} %pad_maximum_fusion.4), channel_id=1, source_target_pairs={{0,16},{1,17},{2,18},{3,19},{4,20},{5,21},{6,22},{7,23},{8,24},{9,... | collective-permute-start | bytes 294920 | tf_op jit(solution)/shard_map/ppermute | solution.py:140
  20.8 48.5 %collective-permute-start.3 = (bf16[4,3,32,128]{3,2,1,0:T(8,128)(2,1)S(1)}, bf16[4,3,32,128]{3,2,1,0:T(8,128)(2,1)S(1)}, u32[]{:S(2)}, u32[]{:S(2)}) collective-permute-start(bf16[4,3,32,128]{3,2,1,0:T(8,128)(2,1)S(1)} %pad_maximum_fusion.4), channel_id=1, source_target_pairs={{0,8},{1,9},{2,10},{3,11},{4,12},{5,13},{6,14},{7,15},{8,16},{9,17... | collective-permute-start | bytes 294920 | tf_op jit(solution)/shard_map/ppermute | solution.py:140
  69.4 19.1 %collective-permute-start.8 = (bf16[4,4,3,32,128]{4,3,2,1,0:T(8,128)(2,1)S(1)}, bf16[4,4,3,32,128]{4,3,2,1,0:T(8,128)(2,1)S(1)}, u32[]{:S(2)}, u32[]{:S(2)}) collective-permute-start(bf16[4,4,3,32,128]{4,3,2,1,0:T(8,128)(2,1)S(1)} %pad_maximum_fusion.1), channel_id=1, source_target_pairs={{0,96},{32,0},{64,32},{96,64},{1,97},{33,1},{65,33},{97,65},{2,98}... | collective-permute-start | bytes 1179656 | tf_op jit(solution)/shard_map/ppermute | solution.py:137
  72.5 16.1 %collective-permute-start.7 = (bf16[4,4,3,32,128]{4,3,2,1,0:T(8,128)(2,1)S(1)}, bf16[4,4,3,32,128]{4,3,2,1,0:T(8,128)(2,1)S(1)}, u32[]{:S(2)}, u32[]{:S(2)}) collective-permute-start(bf16[4,4,3,32,128]{4,3,2,1,0:T(8,128)(2,1)S(1)} %pad_maximum_fusion.1), channel_id=1, source_target_pairs={{0,64},{32,96},{64,0},{96,32},{1,65},{33,97},{65,1},{97,33},{2,66}... | collective-permute-start | bytes 1179656 | tf_op jit(solution)/shard_map/ppermute | solution.py:137
  73.1 19.1 %collective-permute-start.6 = (bf16[4,4,3,32,128]{4,3,2,1,0:T(8,128)(2,1)S(1)}, bf16[4,4,3,32,128]{4,3,2,1,0:T(8,128)(2,1)S(1)}, u32[]{:S(2)}, u32[]{:S(2)}) collective-permute-start(bf16[4,4,3,32,128]{4,3,2,1,0:T(8,128)(2,1)S(1)} %pad_maximum_fusion.1), channel_id=1, source_target_pairs={{0,32},{32,64},{64,96},{96,0},{1,33},{33,65},{65,97},{97,1},{2,34}... | collective-permute-start | bytes 1179656 | tf_op jit(solution)/shard_map/ppermute | solution.py:137
  92.5 7.8 %collective-permute-start.9 = (bf16[4,4,4,3,32,128]{5,4,3,2,1,0:T(8,128)(2,1)S(1)}, bf16[4,4,4,3,32,128]{5,4,3,2,1,0:T(8,128)(2,1)S(1)}, u32[]{:S(2)}, u32[]{:S(2)}) collective-permute-start(bf16[4,4,4,3,32,128]{5,4,3,2,1,0:T(8,128)(2,1)S(1)} %pad_maximum_fusion.mine_ref), channel_id=1, source_target_pairs={{0,1},{1,0},{2,3},{3,2},{4,5},{5,4},{6,7},{7,6},{8,9},{9,8},{10,11... | collective-permute-start | bytes 4718600 | tf_op jit(solution)/shard_map/ppermute | solution.py:146
  92.6 37.2 %all-to-all-start.1 = ((bf16[32,2,1,128,128]{4,3,2,1,0:T(8,128)(2,1)}), bf16[32,2,1,128,128]{4,3,2,1,0:T(8,128)(2,1)}, u32[]{:S(2)}, u32[]{:S(2)}) async-start(bf16[32,2,1,128,128]{4,3,2,1,0:T(8,128)(2,1)} %slice.77), calls=%async_computation.1 | async-start | bytes 4194304 | tf_op jit(solution)/shard_map/all_to_all | solution.py:168
  113.1 27.5 %collective-permute-start.11 = (bf16[4,4,4,32,128]{4,3,2,1,0:T(8,128)(2,1)}, bf16[4,4,4,32,128]{4,3,2,1,0:T(8,128)(2,1)}, u32[]{:S(2)}, u32[]{:S(2)}) collective-permute-start(bf16[4,4,4,32,128]{4,3,2,1,0:T(8,128)(2,1)} %get-tuple-element.31), channel_id=1, source_target_pairs={{0,1},{1,0},{2,3},{3,2},{4,5},{5,4},{6,7},{7,6},{8,9},{9,8},{10,11... | collective-permute-start | bytes 1572872 | tf_op jit(solution)/shard_map/ppermute | solution.py:146
  126.2 15.6 %collective-permute-start.10 = (bf16[4,4,4,32,128]{4,3,2,1,0:T(8,128)(2,1)}, bf16[4,4,4,32,128]{4,3,2,1,0:T(8,128)(2,1)}, u32[]{:S(2)}, u32[]{:S(2)}) collective-permute-start(bf16[4,4,4,32,128]{4,3,2,1,0:T(8,128)(2,1)} %get-tuple-element.29), channel_id=1, source_target_pairs={{0,1},{1,0},{2,3},{3,2},{4,5},{5,4},{6,7},{7,6},{8,9},{9,8},{10,11... | collective-permute-start | bytes 1572872 | tf_op jit(solution)/shard_map/ppermute | solution.py:146
  140.5 6.0 %collective-permute-start.15 = (bf16[4,4,4,32,128]{4,3,2,1,0:T(8,128)(2,1)S(1)}, bf16[4,4,4,32,128]{4,3,2,1,0:T(8,128)(2,1)S(1)}, u32[]{:S(2)}, u32[]{:S(2)}) collective-permute-start(bf16[4,4,4,32,128]{4,3,2,1,0:T(8,128)(2,1)S(1)} %get-tuple-element.34), channel_id=1, source_target_pairs={{0,1},{1,0},{2,3},{3,2},{4,5},{5,4},{6,7},{7,6},{8,9},{9,8},{10,11... | collective-permute-start | bytes 1572872 | tf_op jit(solution)/shard_map/ppermute | solution.py:146
  143.2 16.1 %collective-permute-start.12 = (bf16[4,4,2,32,128]{4,3,1,0,2:T(8,128)(2,1)S(1)}, bf16[4,4,2,32,128]{4,3,1,0,2:T(8,128)(2,1)S(1)}, u32[]{:S(2)}, u32[]{:S(2)}) collective-permute-start(bf16[4,4,2,32,128]{4,3,1,0,2:T(8,128)(2,1)S(1)} %get-tuple-element.35), channel_id=1, source_target_pairs={{0,32},{32,64},{64,96},{96,0},{1,33},{33,65},{65,97},{97,1},{2,34}... | collective-permute-start | bytes 786440 | tf_op jit(solution)/shard_map/ppermute | solution.py:137
  143.3 16.0 %collective-permute-start.14 = (bf16[4,4,2,32,128]{4,3,1,0,2:T(8,128)(2,1)S(1)}, bf16[4,4,2,32,128]{4,3,1,0,2:T(8,128)(2,1)S(1)}, u32[]{:S(2)}, u32[]{:S(2)}) collective-permute-start(bf16[4,4,2,32,128]{4,3,1,0,2:T(8,128)(2,1)S(1)} %get-tuple-element.36), channel_id=1, source_target_pairs={{0,96},{32,0},{64,32},{96,64},{1,97},{33,1},{65,33},{97,65},{2,98}... | collective-permute-start | bytes 786440 | tf_op jit(solution)/shard_map/ppermute | solution.py:137
  146.5 12.8 %collective-permute-start.13 = (bf16[4,4,2,32,128]{4,3,1,0,2:T(8,128)(2,1)S(1)}, bf16[4,4,2,32,128]{4,3,1,0,2:T(8,128)(2,1)S(1)}, u32[]{:S(2)}, u32[]{:S(2)}) collective-permute-start(bf16[4,4,2,32,128]{4,3,1,0,2:T(8,128)(2,1)S(1)} %get-tuple-element.37), channel_id=1, source_target_pairs={{0,64},{32,96},{64,0},{96,32},{1,65},{33,97},{65,1},{97,33},{2,66}... | collective-permute-start | bytes 786440 | tf_op jit(solution)/shard_map/ppermute | solution.py:137
  146.7 14.9 %collective-permute-start.16 = (bf16[4,4,1,32,128]{4,3,1,0,2:T(8,128)(2,1)S(1)}, bf16[4,4,1,32,128]{4,3,1,0,2:T(8,128)(2,1)S(1)}, u32[]{:S(2)}, u32[]{:S(2)}) collective-permute-start(bf16[4,4,1,32,128]{4,3,1,0,2:T(8,128)(2,1)S(1)} %get-tuple-element.38), channel_id=1, source_target_pairs={{0,32},{32,64},{64,96},{96,0},{1,33},{33,65},{65,97},{97,1},{2,34}... | collective-permute-start | bytes 393224 | tf_op jit(solution)/shard_map/ppermute | solution.py:137
  147.6 16.0 %collective-permute-start.18 = (bf16[4,4,1,32,128]{4,3,1,0,2:T(8,128)(2,1)S(1)}, bf16[4,4,1,32,128]{4,3,1,0,2:T(8,128)(2,1)S(1)}, u32[]{:S(2)}, u32[]{:S(2)}) collective-permute-start(bf16[4,4,1,32,128]{4,3,1,0,2:T(8,128)(2,1)S(1)} %get-tuple-element.39), channel_id=1, source_target_pairs={{0,96},{32,0},{64,32},{96,64},{1,97},{33,1},{65,33},{97,65},{2,98}... | collective-permute-start | bytes 393224 | tf_op jit(solution)/shard_map/ppermute | solution.py:137
  159.3 6.5 %collective-permute-start.17 = (bf16[4,4,1,32,128]{4,3,1,0,2:T(8,128)(2,1)S(1)}, bf16[4,4,1,32,128]{4,3,1,0,2:T(8,128)(2,1)S(1)}, u32[]{:S(2)}, u32[]{:S(2)}) collective-permute-start(bf16[4,4,1,32,128]{4,3,1,0,2:T(8,128)(2,1)S(1)} %get-tuple-element.40), channel_id=1, source_target_pairs={{0,64},{32,96},{64,0},{96,32},{1,65},{33,97},{65,1},{97,33},{2,66}... | collective-permute-start | bytes 393224 | tf_op jit(solution)/shard_map/ppermute | solution.py:137
  165.8 6.9 %collective-permute-start.19 = (bf16[4,3,32,128]{3,2,0,1:T(8,128)(2,1)S(1)}, bf16[4,3,32,128]{3,2,0,1:T(8,128)(2,1)S(1)}, u32[]{:S(2)}, u32[]{:S(2)}) collective-permute-start(bf16[4,3,32,128]{3,2,0,1:T(8,128)(2,1)S(1)} %get-tuple-element.41), channel_id=1, source_target_pairs={{0,8},{1,9},{2,10},{3,11},{4,12},{5,13},{6,14},{7,15},{8,16},{9,17... | collective-permute-start | bytes 294920 | tf_op jit(solution)/shard_map/ppermute | solution.py:140
  165.9 6.8 %collective-permute-start.21 = (bf16[4,3,32,128]{3,2,0,1:T(8,128)(2,1)S(1)}, bf16[4,3,32,128]{3,2,0,1:T(8,128)(2,1)S(1)}, u32[]{:S(2)}, u32[]{:S(2)}) collective-permute-start(bf16[4,3,32,128]{3,2,0,1:T(8,128)(2,1)S(1)} %get-tuple-element.42), channel_id=1, source_target_pairs={{0,24},{1,25},{2,26},{3,27},{4,28},{5,29},{6,30},{7,31},{8,0},{9,1... | collective-permute-start | bytes 294920 | tf_op jit(solution)/shard_map/ppermute | solution.py:140
  169.2 6.1 %collective-permute-start.20 = (bf16[4,3,32,128]{3,2,0,1:T(8,128)(2,1)S(1)}, bf16[4,3,32,128]{3,2,0,1:T(8,128)(2,1)S(1)}, u32[]{:S(2)}, u32[]{:S(2)}) collective-permute-start(bf16[4,3,32,128]{3,2,0,1:T(8,128)(2,1)S(1)} %get-tuple-element.43), channel_id=1, source_target_pairs={{0,16},{1,17},{2,18},{3,19},{4,20},{5,21},{6,22},{7,23},{8,24},{9,... | collective-permute-start | bytes 294920 | tf_op jit(solution)/shard_map/ppermute | solution.py:140
  (11 other events, 56.4 us)

commit v4 on v3

--- a/solution.py
+++ b/solution.py
@@ -12,28 +12,34 @@
 F32 = jnp.float32
 CORES = 2
 FLOOR = 2
-UNROLL = 4
+UNROLL = 8
+LIFT_UNROLL = 4
 
 
 def member_kernel(
     where_ref, cols_ref, ens_ref, mine_ref, other_ref, vt_ref, vn_ref, mask_ref, tiles_ref,
-    near_ref, far_ref, tile_buf, lifted, spread_buf, sems, *, var, slot_of_var,
+    near_ref, far_ref, ens_buf, tile_buf, lifted, spread_buf, ens_sems, tile_sems, *, var, slot_of_var,
 ):
-    members = ens_ref.shape[1]
-    n_blocks = ens_ref.shape[0]
-    levels = ens_ref.shape[3]
-    width = ens_ref.shape[4]
+    n_blocks, members, levels, width = ens_buf.shape
     y_n, z_n, x_n = mine_ref.shape[0], mine_ref.shape[1], mine_ref.shape[2]
     part_l = mine_ref.shape[4]
     slots = cols_ref.shape[1]
     my_y, my_z, my_x, my_c = where_ref[0], where_ref[1], where_ref[2], where_ref[3]
-    n_copies = sems.shape[0]
+    n_copies = z_n
     per_copy = n_blocks // n_copies
+
+    def ens_copy(off_z):
+        span = pl.ds(lax.rem(my_z + off_z, z_n) * per_copy, per_copy)
+        return pltpu.make_async_copy(
+            ens_ref.at[span, :, slot_of_var], ens_buf.at[span], ens_sems.at[off_z]
+        )
 
     def tile_copy(piece):
         span = pl.ds(piece * per_copy, per_copy)
-        return pltpu.make_async_copy(tiles_ref.at[span], tile_buf.at[span], sems.at[piece])
-
+        return pltpu.make_async_copy(tiles_ref.at[span], tile_buf.at[span], tile_sems.at[piece])
+
+    for piece in range(n_copies):
+        ens_copy(piece).start()
     for piece in range(n_copies):
         tile_copy(piece).start()
 
@@ -50,7 +56,7 @@
             for quarter in range(y_n):
                 off_y = lax.rem(my_y - quarter + y_n, y_n)
                 incr = source_ref[off_y, in_z, in_x, var].astype(F32)
-                rows = ens_ref[block, m, slot_of_var, quarter * part_l:(quarter + 1) * part_l, :]
+                rows = ens_buf[block, m, quarter * part_l:(quarter + 1) * part_l, :]
                 bands.append((rows.astype(F32) * incr).astype(BF))
             halves.append(jnp.concatenate(bands, axis=0))
         weighted = jnp.concatenate(halves, axis=1)
@@ -68,9 +74,9 @@
         lift_block(other_ref, base + 1 - my_c, in_z, in_x)
         return carry
 
-    lax.fori_loop(0, n_blocks // CORES, lift_step, 0, unroll=2)
-    for piece in range(n_copies):
-        tile_copy(piece).wait()
+    for off_z in range(z_n):
+        ens_copy(off_z).wait()
+        lax.fori_loop(off_z * x_n, (off_z + 1) * x_n, lift_step, 0, unroll=LIFT_UNROLL)
 
     def spread_block(block):
         parts = []
@@ -89,7 +95,9 @@
         spread_block(step)
         return carry
 
-    lax.fori_loop(0, n_blocks, spread_step, 0, unroll=UNROLL)
+    for piece in range(n_copies):
+        tile_copy(piece).wait()
+        lax.fori_loop(piece * per_copy, (piece + 1) * per_copy, spread_step, 0, unroll=UNROLL)
 
     def lower_block(target_ref, block, off_z, off_x):
         beside = spread_buf[block]
@@ -98,7 +106,7 @@
         )
         total = None
         for m in range(members):
-            term = ens_ref[block, m, slot_of_var].astype(F32) * lowered[:, m * width:(m + 1) * width]
+            term = ens_buf[block, m].astype(F32) * lowered[:, m * width:(m + 1) * width]
             total = term if total is None else total + term
         total = total.astype(BF)
         for quarter in range(y_n):
@@ -111,7 +119,7 @@
         lower_block(far_ref, base + 1 - my_c, off_z, off_x)
         return carry
 
-    lax.fori_loop(0, n_blocks // CORES, lower_step, 0, unroll=2)
+    lax.fori_loop(0, n_blocks // CORES, lower_step, 0, unroll=8)
 
 
 def on_device(
@@ -175,6 +183,7 @@
 
     vmem = pl.BlockSpec(memory_space=pltpu.VMEM)
     smem = pl.BlockSpec(memory_space=pltpu.SMEM)
+    anywhere = pl.BlockSpec(memory_space=pl.ANY)
     out = jax.ShapeDtypeStruct((y_n, z_n, x_n, part_l, width), BF)
 
     def add(parts):
@@ -193,14 +202,16 @@
         near, far = pl.pallas_call(
             functools.partial(member_kernel, var=var, slot_of_var=place),
             out_shape=(out, out),
-            in_specs=[smem, smem, vmem, vmem, vmem, vmem, vmem, vmem,
-                      pl.BlockSpec(memory_space=pl.ANY)],
+            in_specs=[smem, smem, anywhere, vmem, vmem, vmem, vmem, vmem,
+                      anywhere],
             out_specs=(vmem, vmem),
             scratch_shapes=[
+                pltpu.VMEM((columns, members, levels, width), BF),
                 pltpu.VMEM(turned_tiles.shape, BF),
                 pltpu.VMEM((columns, width, members * levels), BF),
                 pltpu.VMEM((columns, members * width, levels), BF),
-                pltpu.SemaphoreType.DMA((4,)),
+                pltpu.SemaphoreType.DMA((z_n,)),
+                pltpu.SemaphoreType.DMA((z_n,)),
             ],
             compiler_params=pltpu.CompilerParams(vmem_limit_bytes=40 << 20),
         )(where, tile_col, arrived[index], mine, other, vert_t, vert_root, mask, turned_tiles)

time: 185 us -> 184 us (level)
  Pallas kernels: 34.9 us -> 28 us
  waiting for transfers between devices: 81 us -> 86.1 us
    pallas_call x3, Pallas kernels: 34.9 us -> 28 us  [on_device(): pl.pallas_call(functools.partial(member_kernel, var=var, slot_of_var=plac...]
    all_to_all x1, waiting for transfers between devices: 3.27 us -> 8.41 us  [on_device(): arrived.append(lax.all_to_all(pieces[1], 'col', 0, 0))]
  transfers between devices with their start and end apart: 27 -> 27, of which waited for: 14 -> 14; matrix products, arithmetic and copies ran while one was open for 13% -> 13% of each run, Pallas kernels for 19% -> 15%
where the time goes in v4:
time: 184 us; the launch traced here: 183 us
  waiting for transfers between devices  86.1 us (47%)
  starting transfers between devices  42.6 us (23%)
  Pallas kernels  28 us (15%)
  local copies, waits for them, and re-layouts  21.8 us (12%)
  other arithmetic  4 us (2%)
    ppermute x6, waiting for transfers between devices, shift_z(): lax.ppermute(a, 'col', [(seat(*p), seat(p[0] + s, p[1], p[2])) for p in s...  50.6 us
    pallas_call x3, Pallas kernels, on_device(): pl.pallas_call(functools.partial(member_kernel, var=var, slot_of_var=plac...  28 us
    ppermute x9, waiting for transfers between devices, shift_y(): return lax.ppermute(a, 'mem', [(i, (i + s) % y_n) for i in range(y_n)])  21.8 us
    reshape x1, local copies, waits for them, and re-layouts, on_device(): jnp.transpose(tiles, (0, 3, 1, 2)).reshape(columns, width, slots * width)  11.9 us
    ppermute x9, starting transfers between devices, shift_y(): return lax.ppermute(a, 'mem', [(i, (i + s) % y_n) for i in range(y_n)])  11.3 us
    ppermute x6, starting transfers between devices, shift_x(): lax.ppermute(a, 'col', [(seat(*p), seat(p[0], p[1] + s, p[2])) for p in s...  8.46 us
    all_to_all x1, waiting for transfers between devices, on_device(): arrived.append(lax.all_to_all(pieces[1], 'col', 0, 0))  8.41 us
    ppermute x6, starting transfers between devices, shift_z(): lax.ppermute(a, 'col', [(seat(*p), seat(p[0] + s, p[1], p[2])) for p in s...  8.02 us
  transfers between devices with their start and end apart: 27, of which 14 were waited for; matrix products, arithmetic and copies ran while one was open for 13% of the time, Pallas kernels for 15%

profile of v4, /device:TPU:0, one launch (start us, length us, event | category | flops | bytes accessed | tf_op | source)
XLA Modules:
  0.0 182.9 jit_solution(12137751701486313782)
XLA Ops:
  5.2 4.7 %slice.76 = bf16[32,2,2,128,128]{4,3,2,1,0:T(8,128)(2,1)} slice(bf16[32,2,3,128,128]{4,3,2,1,0:T(8,128)(2,1)} %bitcast.91), slice={[0:32], [0:2], [0:2], [0:128], [0:128]} | slice | bytes 8388608 | tf_op jit(solution)/shard_map/slice | solution.py:161
  9.9 7.0 %all-to-all-start = ((bf16[32,2,2,128,128]{4,3,2,1,0:T(8,128)(2,1)}), bf16[32,2,2,128,128]{4,3,2,1,0:T(8,128)(2,1)}, u32[]{:S(2)}, u32[]{:S(2)}) async-start(bf16[32,2,2,128,128]{4,3,2,1,0:T(8,128)(2,1)} %slice.76), calls=%async_computation | async-start | bytes 8388608 | tf_op jit(solution)/shard_map/all_to_all | solution.py:169
  16.9 3.0 %collective-permute-start.5 = (bf16[4,3,32,128]{3,2,1,0:T(8,128)(2,1)S(1)}, bf16[4,3,32,128]{3,2,1,0:T(8,128)(2,1)S(1)}, u32[]{:S(2)}, u32[]{:S(2)}) collective-permute-start(bf16[4,3,32,128]{3,2,1,0:T(8,128)(2,1)S(1)} %pad_maximum_fusion.4), channel_id=1, source_target_pairs={{0,24},{1,25},{2,26},{3,27},{4,28},{5,29},{6,30},{7,31},{8,0},{9,1... | collective-permute-start | bytes 294920 | tf_op jit(solution)/shard_map/ppermute | solution.py:148
  21.7 3.2 %slice.77 = bf16[32,2,1,128,128]{4,3,2,1,0:T(8,128)(2,1)} slice(bf16[32,2,3,128,128]{4,3,2,1,0:T(8,128)(2,1)} %bitcast.92), slice={[0:32], [0:2], [2:3], [0:128], [0:128]} | slice | bytes 4194304 | tf_op jit(solution)/shard_map/slice | solution.py:161
  24.9 42.0 %collective-permute-done.5 = bf16[4,3,32,128]{3,2,1,0:T(8,128)(2,1)S(1)} collective-permute-done((bf16[4,3,32,128]{3,2,1,0:T(8,128)(2,1)S(1)}, bf16[4,3,32,128]{3,2,1,0:T(8,128)(2,1)S(1)}, u32[]{:S(2)}, u32[]{:S(2)}) %collective-permute-start.5) | collective-permute-done | bytes 98336 | tf_op jit(solution)/shard_map/ppermute | solution.py:148
  69.4 3.1 %collective-permute-start.8 = (bf16[4,4,3,32,128]{4,3,2,1,0:T(8,128)(2,1)S(1)}, bf16[4,4,3,32,128]{4,3,2,1,0:T(8,128)(2,1)S(1)}, u32[]{:S(2)}, u32[]{:S(2)}) collective-permute-start(bf16[4,4,3,32,128]{4,3,2,1,0:T(8,128)(2,1)S(1)} %pad_maximum_fusion.1), channel_id=1, source_target_pairs={{0,96},{32,0},{64,32},{96,64},{1,97},{33,1},{65,33},{97,65},{2,98}... | collective-permute-start | bytes 1179656 | tf_op jit(solution)/shard_map/ppermute | solution.py:145
  74.1 11.9 %copy.38.tiles_ref = bf16[32,128,1024]{2,1,0:T(8,128)(2,1)} copy(bf16[32,128,1024]{1,2,0:T(8,128)(2,1)} %bitcast.90) | data formatting | bytes 16777216 | tf_op jit(solution)/shard_map/reshape | solution.py:171
  86.0 2.5 %collective-permute-done.8 = bf16[4,4,3,32,128]{4,3,2,1,0:T(8,128)(2,1)S(1)} collective-permute-done((bf16[4,4,3,32,128]{4,3,2,1,0:T(8,128)(2,1)S(1)}, bf16[4,4,3,32,128]{4,3,2,1,0:T(8,128)(2,1)S(1)}, u32[]{:S(2)}, u32[]{:S(2)}) %collective-permute-start.8) | collective-permute-done | bytes 393248 | tf_op jit(solution)/shard_map/ppermute | solution.py:145
  88.5 3.7 %collective-permute-done.6 = bf16[4,4,3,32,128]{4,3,2,1,0:T(8,128)(2,1)S(1)} collective-permute-done((bf16[4,4,3,32,128]{4,3,2,1,0:T(8,128)(2,1)S(1)}, bf16[4,4,3,32,128]{4,3,2,1,0:T(8,128)(2,1)S(1)}, u32[]{:S(2)}, u32[]{:S(2)}) %collective-permute-start.6) | collective-permute-done | bytes 393248 | tf_op jit(solution)/shard_map/ppermute | solution.py:145
  92.6 7.2 %all-to-all-start.1 = ((bf16[32,2,1,128,128]{4,3,2,1,0:T(8,128)(2,1)}), bf16[32,2,1,128,128]{4,3,2,1,0:T(8,128)(2,1)}, u32[]{:S(2)}, u32[]{:S(2)}) async-start(bf16[32,2,1,128,128]{4,3,2,1,0:T(8,128)(2,1)} %slice.77), calls=%async_computation.1 | async-start | bytes 4194304 | tf_op jit(solution)/shard_map/all_to_all | solution.py:176
  100.2 9.8 %shard_map.65 = (bf16[4,4,4,32,128]{4,3,2,1,0:T(8,128)(2,1)S(1)}, bf16[4,4,4,32,128]{4,3,2,1,0:T(8,128)(2,1)}) custom-call(s32[4]{0:T(128)S(1)} %pad_add_fusion.where_ref, s32[32,8]{1,0:T(8,128)S(1)} %copy.23.cols_ref, bf16[32,2,2,128,128]{4,3,2,1,0:T(8,128)(2,1)} %all-to-all-done.ens_ref, bf16[4,4,4,3,32,128]{5,4,3,2,1,0:T(8,128)(2,1)S(1)} %pad_maximum_fusion.mine_ref, ...), custom_call_target="tpu_custom_call" | custom-call | tf_op jit(solution)/shard_map/pallas_call | solution.py:202
  111.1 9.2 %shard_map.64 = (bf16[4,4,4,32,128]{4,3,2,1,0:T(8,128)(2,1)S(1)}, bf16[4,4,4,32,128]{4,3,2,1,0:T(8,128)(2,1)}) custom-call(s32[4]{0:T(128)S(1)} %pad_add_fusion.where_ref, s32[32,8]{1,0:T(8,128)S(1)} %copy.23.cols_ref, bf16[32,2,2,128,128]{4,3,2,1,0:T(8,128)(2,1)} %all-to-all-done.ens_ref, bf16[4,4,4,3,32,128]{5,4,3,2,1,0:T(8,128)(2,1)S(1)} %pad_maximum_fusion.mine_ref, ...), custom_call_target="tpu_custom_call" | custom-call | tf_op jit(solution)/shard_map/pallas_call | solution.py:202
  121.4 8.4 %all-to-all-done.1.ens_ref = bf16[32,2,1,128,128]{4,3,2,1,0:T(8,128)(2,1)} async-done(((bf16[32,2,1,128,128]{4,3,2,1,0:T(8,128)(2,1)}), bf16[32,2,1,128,128]{4,3,2,1,0:T(8,128)(2,1)}, u32[]{:S(2)}, u32[]{:S(2)}) %all-to-all-start.1) | async-done | bytes 2097184 | tf_op jit(solution)/shard_map/all_to_all | solution.py:176
  129.8 9.0 %shard_map.66 = (bf16[4,4,4,32,128]{4,3,2,1,0:T(8,128)(2,1)S(1)}, bf16[4,4,4,32,128]{4,3,2,1,0:T(8,128)(2,1)S(1)}) custom-call(s32[4]{0:T(128)S(1)} %pad_add_fusion.where_ref, s32[32,8]{1,0:T(8,128)S(1)} %copy.23.cols_ref, bf16[32,2,1,128,128]{4,3,2,1,0:T(8,128)(2,1)} %all-to-all-done.1.ens_ref, ...), custom_call_target="tpu_custom_call" | custom-call | tf_op jit(solution)/shard_map/pallas_call | solution.py:202
  141.5 3.2 %collective-permute-start.14 = (bf16[4,4,2,32,128]{4,3,1,0,2:T(8,128)(2,1)S(1)}, bf16[4,4,2,32,128]{4,3,1,0,2:T(8,128)(2,1)S(1)}, u32[]{:S(2)}, u32[]{:S(2)}) collective-permute-start(bf16[4,4,2,32,128]{4,3,1,0,2:T(8,128)(2,1)S(1)} %get-tuple-element.36), channel_id=1, source_target_pairs={{0,96},{32,0},{64,32},{96,64},{1,97},{33,1},{65,33},{97,65},{2,98}... | collective-permute-start | bytes 786440 | tf_op jit(solution)/shard_map/ppermute | solution.py:145
  145.9 2.4 %collective-permute-start.18 = (bf16[4,4,1,32,128]{4,3,1,0,2:T(8,128)(2,1)S(1)}, bf16[4,4,1,32,128]{4,3,1,0,2:T(8,128)(2,1)S(1)}, u32[]{:S(2)}, u32[]{:S(2)}) collective-permute-start(bf16[4,4,1,32,128]{4,3,1,0,2:T(8,128)(2,1)S(1)} %get-tuple-element.39), channel_id=1, source_target_pairs={{0,96},{32,0},{64,32},{96,64},{1,97},{33,1},{65,33},{97,65},{2,98}... | collective-permute-start | bytes 393224 | tf_op jit(solution)/shard_map/ppermute | solution.py:145
  148.3 9.3 %collective-permute-done.12 = bf16[4,4,2,32,128]{4,3,1,0,2:T(8,128)(2,1)S(1)} collective-permute-done((bf16[4,4,2,32,128]{4,3,1,0,2:T(8,128)(2,1)S(1)}, bf16[4,4,2,32,128]{4,3,1,0,2:T(8,128)(2,1)S(1)}, u32[]{:S(2)}, u32[]{:S(2)}) %collective-permute-start.12) | collective-permute-done | bytes 262176 | tf_op jit(solution)/shard_map/ppermute | solution.py:145
  157.7 2.1 %collective-permute-done.16 = bf16[4,4,1,32,128]{4,3,1,0,2:T(8,128)(2,1)S(1)} collective-permute-done((bf16[4,4,1,32,128]{4,3,1,0,2:T(8,128)(2,1)S(1)}, bf16[4,4,1,32,128]{4,3,1,0,2:T(8,128)(2,1)S(1)}, u32[]{:S(2)}, u32[]{:S(2)}) %collective-permute-start.16) | collective-permute-done | bytes 131104 | tf_op jit(solution)/shard_map/ppermute | solution.py:145
  161.9 2.1 %collective-permute-done.17 = bf16[4,4,1,32,128]{4,3,1,0,2:T(8,128)(2,1)S(1)} collective-permute-done((bf16[4,4,1,32,128]{4,3,1,0,2:T(8,128)(2,1)S(1)}, bf16[4,4,1,32,128]{4,3,1,0,2:T(8,128)(2,1)S(1)}, u32[]{:S(2)}, u32[]{:S(2)}) %collective-permute-start.17) | collective-permute-done | bytes 131104 | tf_op jit(solution)/shard_map/ppermute | solution.py:145
  164.2 3.2 %collective-permute-start.21 = (bf16[4,3,32,128]{3,2,0,1:T(8,128)(2,1)S(1)}, bf16[4,3,32,128]{3,2,0,1:T(8,128)(2,1)S(1)}, u32[]{:S(2)}, u32[]{:S(2)}) collective-permute-start(bf16[4,3,32,128]{3,2,0,1:T(8,128)(2,1)S(1)} %get-tuple-element.42), channel_id=1, source_target_pairs={{0,24},{1,25},{2,26},{3,27},{4,28},{5,29},{6,30},{7,31},{8,0},{9,1... | collective-permute-start | bytes 294920 | tf_op jit(solution)/shard_map/ppermute | solution.py:148
  167.4 3.6 %collective-permute-done.19 = bf16[4,3,32,128]{3,2,0,1:T(8,128)(2,1)S(1)} collective-permute-done((bf16[4,3,32,128]{3,2,0,1:T(8,128)(2,1)S(1)}, bf16[4,3,32,128]{3,2,0,1:T(8,128)(2,1)S(1)}, u32[]{:S(2)}, u32[]{:S(2)}) %collective-permute-start.19) | collective-permute-done | bytes 98336 | tf_op jit(solution)/shard_map/ppermute | solution.py:148
  171.0 2.6 %collective-permute-done.20 = bf16[4,3,32,128]{3,2,0,1:T(8,128)(2,1)S(1)} collective-permute-done((bf16[4,3,32,128]{3,2,0,1:T(8,128)(2,1)S(1)}, bf16[4,3,32,128]{3,2,0,1:T(8,128)(2,1)S(1)}, u32[]{:S(2)}, u32[]{:S(2)}) %collective-permute-start.20) | collective-permute-done | bytes 98336 | tf_op jit(solution)/shard_map/ppermute | solution.py:148
  173.7 3.2 %collective-permute-start.24 = (bf16[3,32,128]{2,1,0:T(8,128)(2,1)S(1)}, bf16[3,32,128]{2,1,0:T(8,128)(2,1)S(1)}, u32[]{:S(2)}, u32[]{:S(2)}) collective-permute-start(bf16[3,32,128]{2,1,0:T(8,128)(2,1)S(1)} %get-tuple-element.45), channel_id=1, source_target_pairs={{0,6},{1,7},{2,0},{3,1},{4,2},{5,3},{6,4},{7,5},{8,14},{9,15},{10,... | collective-permute-start | bytes 73736 | tf_op jit(solution)/shard_map/ppermute | solution.py:151
  178.7 3.5 %collective-permute-done.23 = bf16[3,32,128]{2,1,0:T(8,128)(2,1)S(1)} collective-permute-done((bf16[3,32,128]{2,1,0:T(8,128)(2,1)S(1)}, bf16[3,32,128]{2,1,0:T(8,128)(2,1)S(1)}, u32[]{:S(2)}, u32[]{:S(2)}) %collective-permute-start.23) | collective-permute-done | bytes 24608 | tf_op jit(solution)/shard_map/ppermute | solution.py:151
  (73 shorter events, 22.6 us)
Async XLA Ops:
  0.0 9.9 %collective-permute-start = (bf16[3,32,128]{2,1,0:T(8,128)(2,1)}, bf16[3,32,128]{2,1,0:T(8,128)(2,1)S(1)}, u32[]{:S(2)}, u32[]{:S(2)}) collective-permute-start(bf16[3,32,128]{2,1,0:T(8,128)(2,1)} %param.7), channel_id=1, source_target_pairs={{0,2},{1,3},{2,4},{3,5},{4,6},{5,7},{6,0},{7,1},{8,10},{9,11},{10,... | collective-permute-start | bytes 73736 | tf_op jit(solution)/shard_map/ppermute | solution.py:151
  1.6 8.3 %collective-permute-start.2 = (bf16[3,32,128]{2,1,0:T(8,128)(2,1)}, bf16[3,32,128]{2,1,0:T(8,128)(2,1)S(1)}, u32[]{:S(2)}, u32[]{:S(2)}) collective-permute-start(bf16[3,32,128]{2,1,0:T(8,128)(2,1)} %param.7), channel_id=1, source_target_pairs={{0,6},{1,7},{2,0},{3,1},{4,2},{5,3},{6,4},{7,5},{8,14},{9,15},{10,... | collective-permute-start | bytes 73736 | tf_op jit(solution)/shard_map/ppermute | solution.py:151
  3.2 6.7 %collective-permute-start.1 = (bf16[3,32,128]{2,1,0:T(8,128)(2,1)}, bf16[3,32,128]{2,1,0:T(8,128)(2,1)S(1)}, u32[]{:S(2)}, u32[]{:S(2)}) collective-permute-start(bf16[3,32,128]{2,1,0:T(8,128)(2,1)} %param.7), channel_id=1, source_target_pairs={{0,4},{1,5},{2,6},{3,7},{4,0},{5,1},{6,2},{7,3},{8,12},{9,13},{10,... | collective-permute-start | bytes 73736 | tf_op jit(solution)/shard_map/ppermute | solution.py:151
  9.9 82.6 %all-to-all-start = ((bf16[32,2,2,128,128]{4,3,2,1,0:T(8,128)(2,1)}), bf16[32,2,2,128,128]{4,3,2,1,0:T(8,128)(2,1)}, u32[]{:S(2)}, u32[]{:S(2)}) async-start(bf16[32,2,2,128,128]{4,3,2,1,0:T(8,128)(2,1)} %slice.76), calls=%async_computation | async-start | bytes 8388608 | tf_op jit(solution)/shard_map/all_to_all | solution.py:169
  16.9 49.9 %collective-permute-start.5 = (bf16[4,3,32,128]{3,2,1,0:T(8,128)(2,1)S(1)}, bf16[4,3,32,128]{3,2,1,0:T(8,128)(2,1)S(1)}, u32[]{:S(2)}, u32[]{:S(2)}) collective-permute-start(bf16[4,3,32,128]{3,2,1,0:T(8,128)(2,1)S(1)} %pad_maximum_fusion.4), channel_id=1, source_target_pairs={{0,24},{1,25},{2,26},{3,27},{4,28},{5,29},{6,30},{7,31},{8,0},{9,1... | collective-permute-start | bytes 294920 | tf_op jit(solution)/shard_map/ppermute | solution.py:148
  20.0 47.4 %collective-permute-start.4 = (bf16[4,3,32,128]{3,2,1,0:T(8,128)(2,1)S(1)}, bf16[4,3,32,128]{3,2,1,0:T(8,128)(2,1)S(1)}, u32[]{:S(2)}, u32[]{:S(2)}) collective-permute-start(bf16[4,3,32,128]{3,2,1,0:T(8,128)(2,1)S(1)} %pad_maximum_fusion.4), channel_id=1, source_target_pairs={{0,16},{1,17},{2,18},{3,19},{4,20},{5,21},{6,22},{7,23},{8,24},{9,... | collective-permute-start | bytes 294920 | tf_op jit(solution)/shard_map/ppermute | solution.py:148
  20.8 48.5 %collective-permute-start.3 = (bf16[4,3,32,128]{3,2,1,0:T(8,128)(2,1)S(1)}, bf16[4,3,32,128]{3,2,1,0:T(8,128)(2,1)S(1)}, u32[]{:S(2)}, u32[]{:S(2)}) collective-permute-start(bf16[4,3,32,128]{3,2,1,0:T(8,128)(2,1)S(1)} %pad_maximum_fusion.4), channel_id=1, source_target_pairs={{0,8},{1,9},{2,10},{3,11},{4,12},{5,13},{6,14},{7,15},{8,16},{9,17... | collective-permute-start | bytes 294920 | tf_op jit(solution)/shard_map/ppermute | solution.py:148
  69.4 19.1 %collective-permute-start.8 = (bf16[4,4,3,32,128]{4,3,2,1,0:T(8,128)(2,1)S(1)}, bf16[4,4,3,32,128]{4,3,2,1,0:T(8,128)(2,1)S(1)}, u32[]{:S(2)}, u32[]{:S(2)}) collective-permute-start(bf16[4,4,3,32,128]{4,3,2,1,0:T(8,128)(2,1)S(1)} %pad_maximum_fusion.1), channel_id=1, source_target_pairs={{0,96},{32,0},{64,32},{96,64},{1,97},{33,1},{65,33},{97,65},{2,98}... | collective-permute-start | bytes 1179656 | tf_op jit(solution)/shard_map/ppermute | solution.py:145
  72.5 16.1 %collective-permute-start.7 = (bf16[4,4,3,32,128]{4,3,2,1,0:T(8,128)(2,1)S(1)}, bf16[4,4,3,32,128]{4,3,2,1,0:T(8,128)(2,1)S(1)}, u32[]{:S(2)}, u32[]{:S(2)}) collective-permute-start(bf16[4,4,3,32,128]{4,3,2,1,0:T(8,128)(2,1)S(1)} %pad_maximum_fusion.1), channel_id=1, source_target_pairs={{0,64},{32,96},{64,0},{96,32},{1,65},{33,97},{65,1},{97,33},{2,66}... | collective-permute-start | bytes 1179656 | tf_op jit(solution)/shard_map/ppermute | solution.py:145
  73.1 19.1 %collective-permute-start.6 = (bf16[4,4,3,32,128]{4,3,2,1,0:T(8,128)(2,1)S(1)}, bf16[4,4,3,32,128]{4,3,2,1,0:T(8,128)(2,1)S(1)}, u32[]{:S(2)}, u32[]{:S(2)}) collective-permute-start(bf16[4,4,3,32,128]{4,3,2,1,0:T(8,128)(2,1)S(1)} %pad_maximum_fusion.1), channel_id=1, source_target_pairs={{0,32},{32,64},{64,96},{96,0},{1,33},{33,65},{65,97},{97,1},{2,34}... | collective-permute-start | bytes 1179656 | tf_op jit(solution)/shard_map/ppermute | solution.py:145
  92.5 7.8 %collective-permute-start.9 = (bf16[4,4,4,3,32,128]{5,4,3,2,1,0:T(8,128)(2,1)S(1)}, bf16[4,4,4,3,32,128]{5,4,3,2,1,0:T(8,128)(2,1)S(1)}, u32[]{:S(2)}, u32[]{:S(2)}) collective-permute-start(bf16[4,4,4,3,32,128]{5,4,3,2,1,0:T(8,128)(2,1)S(1)} %pad_maximum_fusion.mine_ref), channel_id=1, source_target_pairs={{0,1},{1,0},{2,3},{3,2},{4,5},{5,4},{6,7},{7,6},{8,9},{9,8},{10,11... | collective-permute-start | bytes 4718600 | tf_op jit(solution)/shard_map/ppermute | solution.py:154
  92.6 37.2 %all-to-all-start.1 = ((bf16[32,2,1,128,128]{4,3,2,1,0:T(8,128)(2,1)}), bf16[32,2,1,128,128]{4,3,2,1,0:T(8,128)(2,1)}, u32[]{:S(2)}, u32[]{:S(2)}) async-start(bf16[32,2,1,128,128]{4,3,2,1,0:T(8,128)(2,1)} %slice.77), calls=%async_computation.1 | async-start | bytes 4194304 | tf_op jit(solution)/shard_map/all_to_all | solution.py:176
  110.9 28.0 %collective-permute-start.11 = (bf16[4,4,4,32,128]{4,3,2,1,0:T(8,128)(2,1)}, bf16[4,4,4,32,128]{4,3,2,1,0:T(8,128)(2,1)}, u32[]{:S(2)}, u32[]{:S(2)}) collective-permute-start(bf16[4,4,4,32,128]{4,3,2,1,0:T(8,128)(2,1)} %get-tuple-element.31), channel_id=1, source_target_pairs={{0,1},{1,0},{2,3},{3,2},{4,5},{5,4},{6,7},{7,6},{8,9},{9,8},{10,11... | collective-permute-start | bytes 1572872 | tf_op jit(solution)/shard_map/ppermute | solution.py:154
  121.1 19.1 %collective-permute-start.10 = (bf16[4,4,4,32,128]{4,3,2,1,0:T(8,128)(2,1)}, bf16[4,4,4,32,128]{4,3,2,1,0:T(8,128)(2,1)}, u32[]{:S(2)}, u32[]{:S(2)}) collective-permute-start(bf16[4,4,4,32,128]{4,3,2,1,0:T(8,128)(2,1)} %get-tuple-element.29), channel_id=1, source_target_pairs={{0,1},{1,0},{2,3},{3,2},{4,5},{5,4},{6,7},{7,6},{8,9},{9,8},{10,11... | collective-permute-start | bytes 1572872 | tf_op jit(solution)/shard_map/ppermute | solution.py:154
  138.8 6.0 %collective-permute-start.15 = (bf16[4,4,4,32,128]{4,3,2,1,0:T(8,128)(2,1)S(1)}, bf16[4,4,4,32,128]{4,3,2,1,0:T(8,128)(2,1)S(1)}, u32[]{:S(2)}, u32[]{:S(2)}) collective-permute-start(bf16[4,4,4,32,128]{4,3,2,1,0:T(8,128)(2,1)S(1)} %get-tuple-element.34), channel_id=1, source_target_pairs={{0,1},{1,0},{2,3},{3,2},{4,5},{5,4},{6,7},{7,6},{8,9},{9,8},{10,11... | collective-permute-start | bytes 1572872 | tf_op jit(solution)/shard_map/ppermute | solution.py:154
  141.5 16.1 %collective-permute-start.12 = (bf16[4,4,2,32,128]{4,3,1,0,2:T(8,128)(2,1)S(1)}, bf16[4,4,2,32,128]{4,3,1,0,2:T(8,128)(2,1)S(1)}, u32[]{:S(2)}, u32[]{:S(2)}) collective-permute-start(bf16[4,4,2,32,128]{4,3,1,0,2:T(8,128)(2,1)S(1)} %get-tuple-element.35), channel_id=1, source_target_pairs={{0,32},{32,64},{64,96},{96,0},{1,33},{33,65},{65,97},{97,1},{2,34}... | collective-permute-start | bytes 786440 | tf_op jit(solution)/shard_map/ppermute | solution.py:145
  141.5 16.0 %collective-permute-start.14 = (bf16[4,4,2,32,128]{4,3,1,0,2:T(8,128)(2,1)S(1)}, bf16[4,4,2,32,128]{4,3,1,0,2:T(8,128)(2,1)S(1)}, u32[]{:S(2)}, u32[]{:S(2)}) collective-permute-start(bf16[4,4,2,32,128]{4,3,1,0,2:T(8,128)(2,1)S(1)} %get-tuple-element.36), channel_id=1, source_target_pairs={{0,96},{32,0},{64,32},{96,64},{1,97},{33,1},{65,33},{97,65},{2,98}... | collective-permute-start | bytes 786440 | tf_op jit(solution)/shard_map/ppermute | solution.py:145
  144.8 12.8 %collective-permute-start.13 = (bf16[4,4,2,32,128]{4,3,1,0,2:T(8,128)(2,1)S(1)}, bf16[4,4,2,32,128]{4,3,1,0,2:T(8,128)(2,1)S(1)}, u32[]{:S(2)}, u32[]{:S(2)}) collective-permute-start(bf16[4,4,2,32,128]{4,3,1,0,2:T(8,128)(2,1)S(1)} %get-tuple-element.37), channel_id=1, source_target_pairs={{0,64},{32,96},{64,0},{96,32},{1,65},{33,97},{65,1},{97,33},{2,66}... | collective-permute-start | bytes 786440 | tf_op jit(solution)/shard_map/ppermute | solution.py:145
  145.0 14.9 %collective-permute-start.16 = (bf16[4,4,1,32,128]{4,3,1,0,2:T(8,128)(2,1)S(1)}, bf16[4,4,1,32,128]{4,3,1,0,2:T(8,128)(2,1)S(1)}, u32[]{:S(2)}, u32[]{:S(2)}) collective-permute-start(bf16[4,4,1,32,128]{4,3,1,0,2:T(8,128)(2,1)S(1)} %get-tuple-element.38), channel_id=1, source_target_pairs={{0,32},{32,64},{64,96},{96,0},{1,33},{33,65},{65,97},{97,1},{2,34}... | collective-permute-start | bytes 393224 | tf_op jit(solution)/shard_map/ppermute | solution.py:145
  145.9 16.0 %collective-permute-start.18 = (bf16[4,4,1,32,128]{4,3,1,0,2:T(8,128)(2,1)S(1)}, bf16[4,4,1,32,128]{4,3,1,0,2:T(8,128)(2,1)S(1)}, u32[]{:S(2)}, u32[]{:S(2)}) collective-permute-start(bf16[4,4,1,32,128]{4,3,1,0,2:T(8,128)(2,1)S(1)} %get-tuple-element.39), channel_id=1, source_target_pairs={{0,96},{32,0},{64,32},{96,64},{1,97},{33,1},{65,33},{97,65},{2,98}... | collective-permute-start | bytes 393224 | tf_op jit(solution)/shard_map/ppermute | solution.py:145
  157.5 6.5 %collective-permute-start.17 = (bf16[4,4,1,32,128]{4,3,1,0,2:T(8,128)(2,1)S(1)}, bf16[4,4,1,32,128]{4,3,1,0,2:T(8,128)(2,1)S(1)}, u32[]{:S(2)}, u32[]{:S(2)}) collective-permute-start(bf16[4,4,1,32,128]{4,3,1,0,2:T(8,128)(2,1)S(1)} %get-tuple-element.40), channel_id=1, source_target_pairs={{0,64},{32,96},{64,0},{96,32},{1,65},{33,97},{65,1},{97,33},{2,66}... | collective-permute-start | bytes 393224 | tf_op jit(solution)/shard_map/ppermute | solution.py:145
  164.1 6.9 %collective-permute-start.19 = (bf16[4,3,32,128]{3,2,0,1:T(8,128)(2,1)S(1)}, bf16[4,3,32,128]{3,2,0,1:T(8,128)(2,1)S(1)}, u32[]{:S(2)}, u32[]{:S(2)}) collective-permute-start(bf16[4,3,32,128]{3,2,0,1:T(8,128)(2,1)S(1)} %get-tuple-element.41), channel_id=1, source_target_pairs={{0,8},{1,9},{2,10},{3,11},{4,12},{5,13},{6,14},{7,15},{8,16},{9,17... | collective-permute-start | bytes 294920 | tf_op jit(solution)/shard_map/ppermute | solution.py:148
  164.2 6.8 %collective-permute-start.21 = (bf16[4,3,32,128]{3,2,0,1:T(8,128)(2,1)S(1)}, bf16[4,3,32,128]{3,2,0,1:T(8,128)(2,1)S(1)}, u32[]{:S(2)}, u32[]{:S(2)}) collective-permute-start(bf16[4,3,32,128]{3,2,0,1:T(8,128)(2,1)S(1)} %get-tuple-element.42), channel_id=1, source_target_pairs={{0,24},{1,25},{2,26},{3,27},{4,28},{5,29},{6,30},{7,31},{8,0},{9,1... | collective-permute-start | bytes 294920 | tf_op jit(solution)/shard_map/ppermute | solution.py:148
  167.4 6.1 %collective-permute-start.20 = (bf16[4,3,32,128]{3,2,0,1:T(8,128)(2,1)S(1)}, bf16[4,3,32,128]{3,2,0,1:T(8,128)(2,1)S(1)}, u32[]{:S(2)}, u32[]{:S(2)}) collective-permute-start(bf16[4,3,32,128]{3,2,0,1:T(8,128)(2,1)S(1)} %get-tuple-element.43), channel_id=1, source_target_pairs={{0,16},{1,17},{2,18},{3,19},{4,20},{5,21},{6,22},{7,23},{8,24},{9,... | collective-permute-start | bytes 294920 | tf_op jit(solution)/shard_map/ppermute | solution.py:148
  (11 other events, 54.7 us)
